TPU v7x, 32 devices: a whole 2x2x4 slice. The times are simulated.
32 devices in a mesh: dp: 8 (over y, x, core), mp: 4 (over z).
Axes of the slice: x: 2, y: 2, z: 4, core: 2. Of those that a mesh axis runs over, the one named last changes fastest.
Arguments:
- hidden_in: bfloat16 [32, 512, 1024], P('dp', 'mp'), may hold values from -6 to 6
- lengths: int32 [32], P('dp'), may hold values from 128 to 512, as said below
- separators: int32 [32], P('dp'), may hold values from 32 to 383, as said below
- seg_table: float32 [2, 1024], replicated, may hold values from -3 to 3
- query_key_value_weight: bfloat16 [1024, 3, 1024], P('dp', None, 'mp'), may hold values from -0.25 to 0.25
- output_weight: bfloat16 [1024, 1024], P('dp', 'mp'), may hold values from -1.5 to 1.5
- up_weight: bfloat16 [1024, 4096], P('dp', 'mp'), may hold values from -0.1875 to 0.1875
- down_weight: bfloat16 [1024, 4096], P('dp', 'mp'), may hold values from -0.09375 to 0.09375
- bias_q: float32 [1024], replicated, may hold values from -2 to 2
- bias_v: float32 [1024], replicated, may hold values from -0.3 to 0.3
- bias_out: float32 [1024], replicated, may hold values from -2 to 2
- expand_bias: float32 [4096], replicated, may hold values from -2 to 2
- bias_down: float32 [1024], replicated, may hold values from -2 to 2
- gain_attn: float32 [1024], replicated, may hold values from 0.25 to 1.75
- shift_attn: float32 [1024], replicated, may hold values from -2 to 2
- gain_ffn: float32 [1024], replicated, may hold values from 0.25 to 1.75
- shift_ffn: float32 [1024], replicated, may hold values from -2 to 2
- cotangent: bfloat16 [32, 512, 1024], P('dp', 'mp'), may hold values from -8 to 8
Outputs:
- out_hidden: bfloat16 [32, 512, 1024], P('dp', 'mp')
- grad_hidden: bfloat16 [32, 512, 1024], P('dp', 'mp')
- grad_bias_q: float32 [1024], replicated
- grad_bias_v: float32 [1024], replicated
- grad_bias_out: float32 [1024], replicated
- grad_bias_up: float32 [4096], replicated
- grad_bias_down: float32 [1024], replicated
- grad_shift_attn: float32 [1024], replicated
- grad_shift_ffn: float32 [1024], replicated
Inputs may be any that keep to these rules, and one draw needn't show every extreme that they name: `lengths`: every sequence whose index is a multiple of 4 has all 512 tokens, every one whose index is 2 more than a multiple of 4 has 128. `separators`: a separator lies between a quarter and three quarters of its sequence's length.
All inputs are finite; a program needn't handle non-finite values.
Results may differ from a plain program's by a relative error of at most 0.017.
Values may be sent and summed in bfloat16 or wider, within the bound.
A program may use at most 128 MiB of HBM per device.

v0:
```python
import math

import jax
import jax.numpy as jnp
from jax import lax
from jax.sharding import PartitionSpec as P

D = 1024
HEAD_DIM = 64
FF = 4096
SEQ_MB = 1
MICRO = 4


EPS = 1e-12


def layer_norm_parts(values, gain, shift):
    center = values - jnp.mean(values, axis=-1, keepdims=True)
    inverse = lax.rsqrt(jnp.mean(center * center, axis=-1, keepdims=True) + EPS)
    normal = center * inverse
    return (normal * gain + shift, normal, inverse)


def norm_back(grad, normal, inverse, gain):
    scaled = grad * gain
    return inverse * (
        scaled
        - jnp.mean(scaled, axis=-1, keepdims=True)
        - normal * jnp.mean(scaled * normal, axis=-1, keepdims=True)
    )


def masked_scores(query_rows, key_rows, length):
    scores = jnp.einsum("qhd,khd->hqk", query_rows, key_rows, preferred_element_type=jnp.float32)
    valid = jnp.arange(scores.shape[-1], dtype=jnp.int32) < length
    return jnp.where(valid[None, None, :], scores, -1e30)


def attend(pieces):
    query_rows, key_rows, value_rows, length = pieces
    scores = masked_scores(query_rows, key_rows, length)
    highest = jnp.max(scores, axis=-1, keepdims=True)
    expanded = jnp.exp(scores - highest)
    totals = jnp.sum(expanded, axis=-1, keepdims=True)
    weights = (expanded / totals).astype(jnp.bfloat16)
    context_rows = jnp.einsum(
        "hqk,khd->qhd", weights, value_rows, preferred_element_type=jnp.float32
    )
    return (context_rows, highest + jnp.log(totals))


def attend_back(pieces):
    query_rows, key_rows, value_rows, length, log_total, grad_context = pieces
    probs = jnp.exp(masked_scores(query_rows, key_rows, length) - log_total)
    grad_probs = jnp.einsum(
        "qhd,khd->hqk", grad_context, value_rows, preferred_element_type=jnp.float32
    )
    grad_values = jnp.einsum(
        "hqk,qhd->khd", probs.astype(jnp.bfloat16), grad_context, preferred_element_type=jnp.float32
    )
    inner_sum = jnp.sum(probs * grad_probs, axis=-1, keepdims=True)
    grad_scores = (probs * (grad_probs - inner_sum)).astype(jnp.bfloat16)
    grad_queries = jnp.einsum(
        "hqk,khd->qhd", grad_scores, key_rows, preferred_element_type=jnp.float32
    )
    grad_keys = jnp.einsum(
        "hqk,qhd->khd", grad_scores, query_rows, preferred_element_type=jnp.float32
    )
    return (
        grad_queries.astype(jnp.bfloat16),
        grad_keys.astype(jnp.bfloat16),
        grad_values.astype(jnp.bfloat16),
    )


def gelu_exact(inner_value):
    return jax.nn.gelu(inner_value, approximate=False)


def gather_rows(query_key_value_weight, output_weight, up_weight, down_weight):
    return (
        lax.all_gather(query_key_value_weight, "dp", axis=0, tiled=True),
        lax.all_gather(output_weight, "dp", axis=0, tiled=True),
        lax.all_gather(up_weight, "dp", axis=0, tiled=True),
        lax.all_gather(down_weight, "dp", axis=0, tiled=True),
    )


def run_group(hidden_rows, grad_rows, flags, length_rows, fetch, biases, norms):
    bias_q, bias_v, expand_bias = biases
    seg_table, bias_out, bias_down, gain_attn, shift_attn, gain_ffn, shift_ffn = norms
    groups = hidden_rows.shape[0]
    scale = 1.0 / math.sqrt(HEAD_DIM)
    query_key_value_whole, output_weight_whole, up_weight_whole, down_weight_whole = fetch()
    width_here = query_key_value_whole.shape[2]
    heads_here = width_here // HEAD_DIM
    embedded_tokens = (
        hidden_rows.astype(jnp.float32)
        + seg_table[0]
        + flags[..., None] * (seg_table[1] - seg_table[0])
    )
    embedded_low = embedded_tokens.astype(jnp.bfloat16)
    gathered_rows = lax.all_gather(embedded_low, "mp", axis=1, tiled=True)
    seq_len = gathered_rows.shape[1]
    head_shape = (groups, seq_len, heads_here, HEAD_DIM)
    projected_rows = jnp.einsum(
        "tzo,ogv->tzgv", gathered_rows, query_key_value_whole, preferred_element_type=jnp.float32
    )
    queries = ((projected_rows[:, :, 0] + bias_q) * scale).astype(jnp.bfloat16).reshape(head_shape)
    key_rows = projected_rows[:, :, 1].astype(jnp.bfloat16).reshape(head_shape)
    value_rows = (projected_rows[:, :, 2] + bias_v).astype(jnp.bfloat16).reshape(head_shape)
    context_rows, log_total = lax.map(attend, (queries, key_rows, value_rows, length_rows))
    context_reduced = context_rows.reshape(groups, seq_len, width_here).astype(jnp.bfloat16)
    attn_terms = jnp.einsum(
        "mqg,ag->mqa", context_reduced, output_weight_whole, preferred_element_type=jnp.float32
    )
    attended_rows = lax.psum_scatter(attn_terms, "mp", scatter_dimension=1, tiled=True)
    normalized_rows, normal_attn, inv_attn = layer_norm_parts(
        embedded_tokens + attended_rows + bias_out, gain_attn, shift_attn
    )
    normed_low = normalized_rows.astype(jnp.bfloat16)
    spread_input = lax.all_gather(normed_low, "mp", axis=1, tiled=True)
    inner_activation = (
        jnp.einsum("twv,ve->twe", spread_input, up_weight_whole, preferred_element_type=jnp.float32)
        + expand_bias
    )
    active_units = gelu_exact(inner_activation).astype(jnp.bfloat16)
    feedforward_terms = jnp.einsum(
        "jrx,vx->jrv", active_units, down_weight_whole, preferred_element_type=jnp.float32
    )
    feedforward_output = lax.psum_scatter(
        feedforward_terms.astype(jnp.bfloat16), "mp", scatter_dimension=1, tiled=True
    ).astype(jnp.float32)
    result, normal_ffn, inv_ffn = layer_norm_parts(
        normalized_rows + feedforward_output + bias_down, gain_ffn, shift_ffn
    )
    query_key_value_whole, output_weight_whole, up_weight_whole, down_weight_whole = fetch()
    grad_out = grad_rows.astype(jnp.float32)
    grad_mid = norm_back(grad_out, normal_ffn, inv_ffn, gain_ffn)
    grad_mid_low = grad_mid.astype(jnp.bfloat16)
    spread_backward = lax.all_gather(grad_mid_low, "mp", axis=1, tiled=True)
    grad_active = jnp.einsum(
        "twv,ve->twe", spread_backward, down_weight_whole, preferred_element_type=jnp.float32
    )
    gelu_pull = jax.vjp(gelu_exact, inner_activation)[1]
    inner_gradient = gelu_pull(grad_active)[0].astype(jnp.bfloat16)
    expand_terms = jnp.einsum(
        "jrx,vx->jrv", inner_gradient, up_weight_whole, preferred_element_type=jnp.float32
    )
    grad_normed = grad_mid + lax.psum_scatter(
        expand_terms.astype(jnp.bfloat16), "mp", scatter_dimension=1, tiled=True
    ).astype(jnp.float32)
    grad_first = norm_back(grad_normed, normal_attn, inv_attn, gain_attn)
    grad_first_low = grad_first.astype(jnp.bfloat16)
    attention_backward = lax.all_gather(grad_first_low, "mp", axis=1, tiled=True)
    grad_context = jnp.einsum(
        "fox,xn->fon", attention_backward, output_weight_whole, preferred_element_type=jnp.float32
    )
    grad_context = grad_context.astype(jnp.bfloat16).reshape(head_shape)
    grad_queries, grad_keys, grad_values = lax.map(
        attend_back, (queries, key_rows, value_rows, length_rows, log_total, grad_context)
    )
    grad_queries = grad_queries.reshape(groups, seq_len, width_here) * scale
    grad_keys = grad_keys.reshape(groups, seq_len, width_here)
    grad_values = grad_values.reshape(groups, seq_len, width_here)
    stacked_rows = jnp.stack([grad_queries, grad_keys, grad_values], axis=2)
    query_key_value_terms = jnp.einsum(
        "hgax,bax->hgb", stacked_rows, query_key_value_whole, preferred_element_type=jnp.float32
    )
    grad_embedded = grad_first + lax.psum_scatter(
        query_key_value_terms.astype(jnp.bfloat16), "mp", scatter_dimension=1, tiled=True
    ).astype(jnp.float32)
    fresh = [
        jnp.sum(grad_queries.astype(jnp.float32), axis=(0, 1)),
        jnp.sum(grad_values.astype(jnp.float32), axis=(0, 1)),
        jnp.sum(grad_first, axis=(0, 1)),
        jnp.sum(inner_gradient.astype(jnp.float32), axis=(0, 1)),
        jnp.sum(grad_mid, axis=(0, 1)),
        jnp.sum(grad_normed, axis=(0, 1)),
        jnp.sum(grad_out, axis=(0, 1)),
    ]
    return (result.astype(jnp.bfloat16), grad_embedded.astype(jnp.bfloat16), fresh)


def on_device(
    hidden_in,
    lengths,
    separators,
    seg_table,
    query_key_value_weight,
    output_weight,
    up_weight,
    down_weight,
    bias_q,
    bias_v,
    bias_out,
    expand_bias,
    bias_down,
    gain_attn,
    shift_attn,
    gain_ffn,
    shift_ffn,
    cotangent,
):
    model_size = lax.axis_size("mp")
    local_len = hidden_in.shape[1]
    seq_len = local_len * model_size
    total_tokens = hidden_in.shape[0] * seq_len * lax.axis_size("dp")
    norms = (seg_table, bias_out, bias_down, gain_attn, shift_attn, gain_ffn, shift_ffn)
    grad_totals = [
        jnp.zeros((D,), jnp.float32),
        jnp.zeros((D,), jnp.float32),
        jnp.zeros((D,), jnp.float32),
        jnp.zeros((FF,), jnp.float32),
        jnp.zeros((D,), jnp.float32),
        jnp.zeros((D,), jnp.float32),
        jnp.zeros((D,), jnp.float32),
    ]

    def fetch():
        return gather_rows(query_key_value_weight, output_weight, up_weight, down_weight)

    local_width = query_key_value_weight.shape[2]
    local_units = up_weight.shape[1]
    model_index = lax.axis_index("mp")
    biases = (
        lax.dynamic_slice_in_dim(bias_q, model_index * local_width, local_width),
        lax.dynamic_slice_in_dim(bias_v, model_index * local_width, local_width),
        lax.dynamic_slice_in_dim(expand_bias, model_index * local_units, local_units),
    )
    positions = model_index * local_len + jnp.arange(local_len, dtype=jnp.int32)
    seg_flag = (positions[None, :] > separators[:, None]).astype(jnp.float32)
    owner = (jnp.arange(model_size, dtype=jnp.int32) == model_index).astype(jnp.float32)

    def place(piece):
        return (owner[:, None] * piece[None, :]).reshape(-1)

    out_pieces = []
    grad_pieces = []
    for micro in range(MICRO):
        first_row = micro * SEQ_MB
        last_row = first_row + SEQ_MB
        result, grad_embedded, fresh = run_group(
            hidden_in[first_row:last_row],
            cotangent[first_row:last_row],
            seg_flag[first_row:last_row],
            lengths[first_row:last_row],
            fetch,
            biases,
            norms,
        )
        out_pieces.append(result)
        grad_pieces.append(grad_embedded)
        fresh = [
            place(fresh[0]),
            place(fresh[1]),
            fresh[2],
            place(fresh[3]),
            fresh[4],
            fresh[5],
            fresh[6],
        ]
        grad_totals = [held + added for held, added in zip(grad_totals, fresh)]
    out_back = jnp.concatenate(out_pieces, axis=0)
    grad_back = jnp.concatenate(grad_pieces, axis=0)
    summed = lax.psum(
        (
            grad_totals[0],
            grad_totals[1],
            grad_totals[2],
            grad_totals[3],
            grad_totals[4],
            grad_totals[5],
            grad_totals[6],
        ),
        ("dp", "mp"),
    )
    factor = 1.0 / total_tokens
    return (
        out_back,
        grad_back,
        summed[0] * factor,
        summed[1] * factor,
        summed[2] * factor,
        summed[3] * factor,
        summed[4] * factor,
        summed[5] * factor,
        summed[6] * factor,
    )


def solution(mesh):
    placed = (
        P("dp", "mp", None),
        P("dp"),
        P("dp"),
        P(),
        P("dp", None, "mp"),
        P("dp", "mp"),
        P("dp", "mp"),
        P("dp", "mp"),
        P(),
        P(),
        P(),
        P(),
        P(),
        P(),
        P(),
        P(),
        P(),
        P("dp", "mp", None),
    )
    return jax.shard_map(
        on_device,
        mesh=mesh,
        in_specs=placed,
        out_specs=(P("dp", "mp", None), P("dp", "mp", None), P(), P(), P(), P(), P(), P(), P()),
        check_vma=False,
    )
```

profile of v0, /device:TPU:0, one launch (start us, length us, event | category | flops | bytes accessed | tf_op | source)
XLA Modules:
  0.0 1113.0 jit_solution(582167840172878751)
XLA Ops:
  42.1 27.1 %all-gather.22.cloned.1.call-done = bf16[1024,3,256]{0,2,1:T(8,128)(2,1)} async-done(((bf16[128,3,256]{0,2,1:T(8,128)(2,1)}), bf16[1024,3,256]{0,2,1:T(8,128)(2,1)}) %all-gather.22.cloned.1.call-update) | async-done | bytes 1572880 | tf_op jit(solution)/shard_map/all_gather | solution.py:83
  78.6 20.7 %all-gather.30.cloned.1.call-done = bf16[1,512,1024]{2,1,0:T(8,128)(2,1)} async-done(((bf16[1,128,1024]{2,1,0:T(8,128)(2,1)}), bf16[1,512,1024]{2,1,0:T(8,128)(2,1)}) %all-gather.30.cloned.1.call-update) | async-done | bytes 1048592 | tf_op jit(solution)/shard_map/all_gather | solution.py:104
  166.0 36.1 %reduce-scatter.17.cloned.1.call-done = f32[1,128,1024]{2,1,0:T(8,128)} async-done(((f32[1,512,1024]{2,1,0:T(8,128)}), f32[1,128,1024]{2,1,0:T(8,128)}) %reduce-scatter.17.cloned.1.call-update) | async-done | bytes 524304 | tf_op jit(solution)/shard_map/reduce_scatter | solution.py:118
  202.1 45.2 %reduce-scatter.21.cloned.1.call-done = f32[1,128,1024]{2,1,0:T(8,128)} async-done(((f32[1,512,1024]{2,1,0:T(8,128)}), f32[1,128,1024]{2,1,0:T(8,128)}) %reduce-scatter.21.cloned.1.call-update) | async-done | bytes 524304 | tf_op jit(solution)/shard_map/reduce_scatter | solution.py:118
  247.3 45.1 %reduce-scatter.25.cloned.1.call-done = f32[1,128,1024]{2,1,0:T(8,128)} async-done(((f32[1,512,1024]{2,1,0:T(8,128)}), f32[1,128,1024]{2,1,0:T(8,128)}) %reduce-scatter.25.cloned.1.call-update) | async-done | bytes 524304 | tf_op jit(solution)/shard_map/reduce_scatter | solution.py:118
  292.4 45.2 %reduce-scatter.29.cloned.1.call-done = f32[1,128,1024]{2,1,0:T(8,128)} async-done(((f32[1,512,1024]{2,1,0:T(8,128)}), f32[1,128,1024]{2,1,0:T(8,128)}) %reduce-scatter.29.cloned.1.call-update) | async-done | bytes 524304 | tf_op jit(solution)/shard_map/reduce_scatter | solution.py:118
  344.7 21.7 %all-gather.26.cloned.1.call-done = bf16[1024,1024]{1,0:T(8,128)(2,1)} async-done(((bf16[128,1024]{1,0:T(8,128)(2,1)}), bf16[1024,1024]{1,0:T(8,128)(2,1)}) %all-gather.26.cloned.1.call-update) | async-done | bytes 2097168 | tf_op jit(solution)/shard_map/all_gather | solution.py:85
  366.3 29.6 %all-gather.36.cloned.1.call-done = bf16[1,512,1024]{2,1,0:T(8,128)(2,1)} async-done(((bf16[1,128,1024]{2,1,0:T(8,128)(2,1)}), bf16[1,512,1024]{2,1,0:T(8,128)(2,1)}) %all-gather.36.cloned.1.call-update) | async-done | bytes 1048592 | tf_op jit(solution)/shard_map/all_gather | solution.py:123
  400.4 24.9 %all-gather.32.cloned.1.call-done = bf16[1,512,1024]{2,1,0:T(8,128)(2,1)} async-done(((bf16[1,128,1024]{2,1,0:T(8,128)(2,1)}), bf16[1,512,1024]{2,1,0:T(8,128)(2,1)}) %all-gather.32.cloned.1.call-update) | async-done | bytes 1048592 | tf_op jit(solution)/shard_map/all_gather | solution.py:123
  429.8 25.0 %all-gather.24.cloned.1.call-done = bf16[1,512,1024]{2,1,0:T(8,128)(2,1)} async-done(((bf16[1,128,1024]{2,1,0:T(8,128)(2,1)}), bf16[1,512,1024]{2,1,0:T(8,128)(2,1)}) %all-gather.24.cloned.1.call-update) | async-done | bytes 1048592 | tf_op jit(solution)/shard_map/all_gather | solution.py:123
  516.4 28.0 %reduce-scatter.27.cloned.1.call-done = bf16[1,128,1024]{2,1,0:T(8,128)(2,1)} async-done(((bf16[1,512,1024]{2,1,0:T(8,128)(2,1)}), bf16[1,128,1024]{2,1,0:T(8,128)(2,1)}) %reduce-scatter.27.cloned.1.call-update) | async-done | bytes 262160 | tf_op jit(solution)/shard_map/reduce_scatter | solution.py:132
  544.3 28.5 %reduce-scatter.23.cloned.1.call-done = bf16[1,128,1024]{2,1,0:T(8,128)(2,1)} async-done(((bf16[1,512,1024]{2,1,0:T(8,128)(2,1)}), bf16[1,128,1024]{2,1,0:T(8,128)(2,1)}) %reduce-scatter.23.cloned.1.call-update) | async-done | bytes 262160 | tf_op jit(solution)/shard_map/reduce_scatter | solution.py:132
  576.1 26.2 %all-gather.40.cloned.1.call-done = bf16[1,512,1024]{2,1,0:T(8,128)(2,1)} async-done(((bf16[1,128,1024]{2,1,0:T(8,128)(2,1)}), bf16[1,512,1024]{2,1,0:T(8,128)(2,1)}) %all-gather.40.cloned.1.call-update) | async-done | bytes 1048592 | tf_op jit(solution)/shard_map/all_gather | solution.py:123
  615.4 25.3 %reduce-scatter.31.cloned.1.call-done = bf16[1,128,1024]{2,1,0:T(8,128)(2,1)} async-done(((bf16[1,512,1024]{2,1,0:T(8,128)(2,1)}), bf16[1,128,1024]{2,1,0:T(8,128)(2,1)}) %reduce-scatter.31.cloned.1.call-update) | async-done | bytes 262160 | tf_op jit(solution)/shard_map/reduce_scatter | solution.py:132
  680.8 21.1 %all-gather.54.cloned.1.call-done = bf16[1,512,1024]{2,1,0:T(8,128)(2,1)} async-done(((bf16[1,128,1024]{2,1,0:T(8,128)(2,1)}), bf16[1,512,1024]{2,1,0:T(8,128)(2,1)}) %all-gather.54.cloned.1.call-update) | async-done | bytes 1048592 | tf_op jit(solution)/shard_map/all_gather | solution.py:142
  710.1 21.4 %all-gather.42.cloned.1.call-done = bf16[1,512,1024]{2,1,0:T(8,128)(2,1)} async-done(((bf16[1,128,1024]{2,1,0:T(8,128)(2,1)}), bf16[1,512,1024]{2,1,0:T(8,128)(2,1)}) %all-gather.42.cloned.1.call-update) | async-done | bytes 1048592 | tf_op jit(solution)/shard_map/all_gather | solution.py:142
  739.6 20.8 %all-gather.50.cloned.1.call-done = bf16[1,512,1024]{2,1,0:T(8,128)(2,1)} async-done(((bf16[1,128,1024]{2,1,0:T(8,128)(2,1)}), bf16[1,512,1024]{2,1,0:T(8,128)(2,1)}) %all-gather.50.cloned.1.call-update) | async-done | bytes 1048592 | tf_op jit(solution)/shard_map/all_gather | solution.py:142
  768.6 20.6 %reduce-scatter.37.cloned.1.call-done = bf16[1,128,1024]{2,1,0:T(8,128)(2,1)} async-done(((bf16[1,512,1024]{2,1,0:T(8,128)(2,1)}), bf16[1,128,1024]{2,1,0:T(8,128)(2,1)}) %reduce-scatter.37.cloned.1.call-update) | async-done | bytes 262160 | tf_op jit(solution)/shard_map/reduce_scatter | solution.py:151
  789.3 28.7 %reduce-scatter.45.cloned.1.call-done = bf16[1,128,1024]{2,1,0:T(8,128)(2,1)} async-done(((bf16[1,512,1024]{2,1,0:T(8,128)(2,1)}), bf16[1,128,1024]{2,1,0:T(8,128)(2,1)}) %reduce-scatter.45.cloned.1.call-update) | async-done | bytes 262160 | tf_op jit(solution)/shard_map/reduce_scatter | solution.py:151
  818.0 28.5 %reduce-scatter.33.cloned.1.call-done = bf16[1,128,1024]{2,1,0:T(8,128)(2,1)} async-done(((bf16[1,512,1024]{2,1,0:T(8,128)(2,1)}), bf16[1,128,1024]{2,1,0:T(8,128)(2,1)}) %reduce-scatter.33.cloned.1.call-update) | async-done | bytes 262160 | tf_op jit(solution)/shard_map/reduce_scatter | solution.py:151
  854.0 20.4 %reduce-scatter.41.cloned.1.call-done = bf16[1,128,1024]{2,1,0:T(8,128)(2,1)} async-done(((bf16[1,512,1024]{2,1,0:T(8,128)(2,1)}), bf16[1,128,1024]{2,1,0:T(8,128)(2,1)}) %reduce-scatter.41.cloned.1.call-update) | async-done | bytes 262160 | tf_op jit(solution)/shard_map/reduce_scatter | solution.py:151
  882.3 20.2 %all-gather.48.cloned.1.call-done = bf16[1,512,1024]{2,1,0:T(8,128)(2,1)} async-done(((bf16[1,128,1024]{2,1,0:T(8,128)(2,1)}), bf16[1,512,1024]{2,1,0:T(8,128)(2,1)}) %all-gather.48.cloned.1.call-update) | async-done | bytes 1048592 | tf_op jit(solution)/shard_map/all_gather | solution.py:156
  1007.9 42.3 %all-reduce = (f32[1024]{0:T(1024)S(1)}, f32[1024]{0:T(1024)S(1)}, f32[1024]{0:T(1024)S(1)}, f32[4096]{0:T(1024)S(1)}, f32[1024]{0:T(1024)S(1)}, /*index=5*/f32[1024]{0:T(1024)S(1)}, f32[1024]{0:T(1024)S(1)}) all-reduce(f32[1024]{0:T(1024)S(1)} %bitcast.350, f32[1024]{0:T(1024)S(1)} %bitcast.349, ...), channel_id=1, replica_groups=mesh['dp'=8,'mp'=4] {'dp','mp'}, use_global_device_ids=true, to_apply=%region_64.65 | all-reduce | flops 10240 | bytes 81920 | tf_op jit(solution)/shard_map/psum | solution.py:267
  1077.1 27.1 %reduce-scatter.35.cloned.1.call-done = bf16[1,128,1024]{2,1,0:T(8,128)(2,1)} async-done(((bf16[1,512,1024]{2,1,0:T(8,128)(2,1)}), bf16[1,128,1024]{2,1,0:T(8,128)(2,1)}) %reduce-scatter.35.cloned.1.call-update) | async-done | bytes 262160 | tf_op jit(solution)/shard_map/reduce_scatter | solution.py:171
  (465 shorter events, 417.2 us)
Async XLA Ops:
  12.9 115.3 %all-gather.34.cloned.1.call-start = ((), (), s32[]{:S(2)}) async-start(), calls=%async_computation.27 | async-start | bytes 1310720 | tf_op jit(solution)/shard_map/all_gather | solution.py:104
  13.5 143.5 %all-gather.38.cloned.1.call-start = ((), (), s32[]{:S(2)}) async-start(), calls=%async_computation.31 | async-start | bytes 1310720 | tf_op jit(solution)/shard_map/all_gather | solution.py:104
  14.0 188.1 %reduce-scatter.17.cloned.1.call-start = ((), (), s32[]{:S(2)}) async-start(), calls=%async_computation.18 | async-start | bytes 2621440 | tf_op jit(solution)/shard_map/reduce_scatter | solution.py:118
  77.9 169.4 %reduce-scatter.21.cloned.1.call-start = ((), (), s32[]{:S(2)}) async-start(), calls=%async_computation.24 | async-start | bytes 2621440 | tf_op jit(solution)/shard_map/reduce_scatter | solution.py:118
  107.6 184.8 %reduce-scatter.25.cloned.1.call-start = ((), (), s32[]{:S(2)}) async-start(), calls=%async_computation.28 | async-start | bytes 2621440 | tf_op jit(solution)/shard_map/reduce_scatter | solution.py:118
  136.5 201.1 %reduce-scatter.29.cloned.1.call-start = ((), (), s32[]{:S(2)}) async-start(), calls=%async_computation.32 | async-start | bytes 2621440 | tf_op jit(solution)/shard_map/reduce_scatter | solution.py:118
  165.3 201.0 %all-gather.26.cloned.1.call-start = ((), (), s32[]{:S(2)}) async-start(), calls=%async_computation.20 | async-start | bytes 2359296 | tf_op jit(solution)/shard_map/all_gather | solution.py:85
  165.9 230.0 %all-gather.36.cloned.1.call-start = ((), (), s32[]{:S(2)}) async-start(), calls=%async_computation.29 | async-start | bytes 1310720 | tf_op jit(solution)/shard_map/all_gather | solution.py:123
  342.4 112.4 %all-gather.24.cloned.1.call-start = ((), (), s32[]{:S(2)}) async-start(), calls=%async_computation.19 | async-start | bytes 1310720 | tf_op jit(solution)/shard_map/all_gather | solution.py:123
  343.1 140.6 %all-gather.28.cloned.1.call-start = ((), (), s32[]{:S(2)}) async-start(), calls=%async_computation.21 | async-start | bytes 2359296 | tf_op jit(solution)/shard_map/all_gather | solution.py:86
  343.7 172.6 %reduce-scatter.19.cloned.1.call-start = ((), (), s32[]{:S(2)}) async-start(), calls=%async_computation.22 | async-start | bytes 1310720 | tf_op jit(solution)/shard_map/reduce_scatter | solution.py:132
  499.5 102.8 %all-gather.40.cloned.1.call-start = ((), (), s32[]{:S(2)}) async-start(), calls=%async_computation.33 | async-start | bytes 1310720 | tf_op jit(solution)/shard_map/all_gather | solution.py:123
  651.7 108.7 %all-gather.50.cloned.1.call-start = ((), (), s32[]{:S(2)}) async-start(), calls=%async_computation.43 | async-start | bytes 1310720 | tf_op jit(solution)/shard_map/all_gather | solution.py:142
  652.5 136.8 %reduce-scatter.37.cloned.1.call-start = ((), (), s32[]{:S(2)}) async-start(), calls=%async_computation.40 | async-start | bytes 1310720 | tf_op jit(solution)/shard_map/reduce_scatter | solution.py:151
  680.6 137.4 %reduce-scatter.45.cloned.1.call-start = ((), (), s32[]{:S(2)}) async-start(), calls=%async_computation.48 | async-start | bytes 1310720 | tf_op jit(solution)/shard_map/reduce_scatter | solution.py:151
  710.0 136.5 %reduce-scatter.33.cloned.1.call-start = ((), (), s32[]{:S(2)}) async-start(), calls=%async_computation.36 | async-start | bytes 1310720 | tf_op jit(solution)/shard_map/reduce_scatter | solution.py:151
  739.6 134.9 %reduce-scatter.41.cloned.1.call-start = ((), (), s32[]{:S(2)}) async-start(), calls=%async_computation.44 | async-start | bytes 1310720 | tf_op jit(solution)/shard_map/reduce_scatter | solution.py:151
  768.6 133.9 %all-gather.48.cloned.1.call-start = ((), (), s32[]{:S(2)}) async-start(), calls=%async_computation.41 | async-start | bytes 1310720 | tf_op jit(solution)/shard_map/all_gather | solution.py:156
  853.4 107.5 %all-gather.52.cloned.1.call-start = ((), (), s32[]{:S(2)}) async-start(), calls=%async_computation.45 | async-start | bytes 1310720 | tf_op jit(solution)/shard_map/all_gather | solution.py:156
  878.6 111.3 %all-gather.44.cloned.1.call-start = ((), (), s32[]{:S(2)}) async-start(), calls=%async_computation.37 | async-start | bytes 1310720 | tf_op jit(solution)/shard_map/all_gather | solution.py:156
  881.8 176.2 %reduce-scatter.39.cloned.1.call-start = ((), (), s32[]{:S(2)}) async-start(), calls=%async_computation.42 | async-start | bytes 1310720 | tf_op jit(solution)/shard_map/reduce_scatter | solution.py:171
  922.8 136.2 %reduce-scatter.47.cloned.1.call-start = ((), (), s32[]{:S(2)}) async-start(), calls=%async_computation.50 | async-start | bytes 1310720 | tf_op jit(solution)/shard_map/reduce_scatter | solution.py:171
  949.4 126.7 %reduce-scatter.43.cloned.1.call-start = ((), (), s32[]{:S(2)}) async-start(), calls=%async_computation.46 | async-start | bytes 1310720 | tf_op jit(solution)/shard_map/reduce_scatter | solution.py:171
  1000.8 103.4 %reduce-scatter.35.cloned.1.call-start = ((), (), s32[]{:S(2)}) async-start(), calls=%async_computation.38 | async-start | bytes 1310720 | tf_op jit(solution)/shard_map/reduce_scatter | solution.py:171
  (108 other events, 2726.5 us)
Sparse Core Ops, SparseCore 0:
  11.4 30.6 all-gather.19
  71.3 27.9 all-gather.29
  100.8 27.3 all-gather.33
  129.6 27.3 all-gather.37
  159.1 42.9 reduce-scatter.16
  204.4 42.8 reduce-scatter.20
  249.6 42.8 reduce-scatter.24
  294.7 42.8 reduce-scatter.28
  339.3 26.9 all-gather.25
  367.9 27.9 all-gather.35
  397.9 27.3 all-gather.31
  427.4 27.3 all-gather.23
  456.6 27.1 all-gather.27
  489.0 27.2 reduce-scatter.18
  614.0 26.6 reduce-scatter.30
  674.5 27.3 all-gather.53
  704.1 27.3 all-gather.41
  733.0 27.3 all-gather.49
  762.6 26.6 reduce-scatter.36
  876.0 26.4 all-gather.47
  904.7 27.3 all-gather.55
  933.5 27.3 all-gather.51
  962.5 27.3 all-gather.43
  992.2 26.6 reduce-scatter.38
  (11 shorter events, 284.3 us)
where the time goes:
time: 1120 us; the launch traced here: 1110 us
  waiting for transfers between devices  796 us (71%)
  matrix products  161 us (14%)
  other arithmetic  62.3 us (6%)
  blocking collectives  53.7 us (5%)
  local copies, waits for them, and re-layouts  21.1 us (2%)
  between operations  16.1 us (1%)
    reduce_scatter x4, waiting for transfers between devices, run_group(): lax.psum_scatter(attn_terms, 'mp', scatter_dimension=1, tiled=True)  172 us
    all_gather x4, waiting for transfers between devices, run_group(): spread_input = lax.all_gather(normed_low, 'mp', axis=1, tiled=True)  106 us
    reduce_scatter x4, waiting for transfers between devices, run_group(): lax.psum_scatter(feedforward_terms.astype(jnp.bfloat16), 'mp', scatter_di...  98.4 us
    reduce_scatter x4, waiting for transfers between devices, run_group(): lax.psum_scatter(expand_terms.astype(jnp.bfloat16), 'mp', scatter_dimensi...  98.3 us
    all_gather x4, waiting for transfers between devices, run_group(): spread_backward = lax.all_gather(grad_mid_low, 'mp', axis=1, tiled=True)  83.2 us
    all_gather x4, waiting for transfers between devices, run_group(): gathered_rows = lax.all_gather(embedded_low, 'mp', axis=1, tiled=True)  73.8 us
    all_gather x4, waiting for transfers between devices, run_group(): lax.all_gather(grad_first_low, 'mp', axis=1, tiled=True)  55.1 us
    reduce_scatter x4, waiting for transfers between devices, run_group(): lax.psum_scatter(query_key_value_terms.astype(jnp.bfloat16), 'mp', scatte...  43.2 us
  transfers between devices with their start and end apart: 35, of which 33 were waited for; matrix products, arithmetic and copies ran while one was open for 19% of the time, Pallas kernels for 0%

commit v1 on v0

v1 whole, which is shorter than its diff:
```python
import math

import jax
import jax.numpy as jnp
from jax import lax
from jax.sharding import PartitionSpec as P

HEAD_DIM = 64
EPS = 1e-12
F32 = jnp.float32
BF16 = jnp.bfloat16


def norm_parts(values, gain, shift):
    center = values - jnp.mean(values, axis=-1, keepdims=True)
    inverse = lax.rsqrt(jnp.mean(center * center, axis=-1, keepdims=True) + EPS)
    normal = center * inverse
    return normal * gain + shift, normal, inverse


def norm_back(grad, normal, inverse, gain):
    scaled = grad * gain
    return inverse * (
        scaled
        - jnp.mean(scaled, axis=-1, keepdims=True)
        - normal * jnp.mean(scaled * normal, axis=-1, keepdims=True)
    )


def dot(a, b, dims):
    return lax.dot_general(a, b, (dims, ((), ())), preferred_element_type=F32)


def gather_whole(shard):
    rows = lax.all_gather(shard, "dp", axis=0, tiled=True)
    return lax.all_gather(rows, "mp", axis=rows.ndim - 1, tiled=True)


def on_device(
    hidden_in, lengths, separators, seg_table, query_key_value_weight, output_weight, up_weight, down_weight,
    bias_q, bias_v, bias_out, expand_bias, bias_down, gain_attn, shift_attn, gain_ffn, shift_ffn, cotangent,
):
    model_size = lax.axis_size("mp")
    model_index = lax.axis_index("mp")
    here = hidden_in.shape[0] // model_size

    def to_sequences(rows):
        return lax.all_to_all(rows, "mp", split_axis=0, concat_axis=1, tiled=True)

    def to_tokens(rows):
        return lax.all_to_all(rows, "mp", split_axis=1, concat_axis=0, tiled=True)

    hidden = to_sequences(hidden_in)
    grad_rows = to_sequences(cotangent)
    own = model_index * here
    length = lax.dynamic_slice_in_dim(lengths, own, here)
    separator = lax.dynamic_slice_in_dim(separators, own, here)
    wqkv, wo, wup, wdown = (gather_whole(w) for w in (query_key_value_weight, output_weight, up_weight, down_weight))
    seqs, seq_len, width = hidden.shape
    total_tokens = seqs * seq_len * model_size * lax.axis_size("dp")
    heads = width // HEAD_DIM
    scale = 1.0 / math.sqrt(HEAD_DIM)
    positions = jnp.arange(seq_len, dtype=jnp.int32)
    flag = (positions[None, :] > separator[:, None]).astype(F32)
    embedded = hidden.astype(F32) + seg_table[0] + flag[..., None] * (seg_table[1] - seg_table[0])
    low = embedded.astype(BF16)
    projected = jnp.einsum("tzo,ogv->gtzv", low, wqkv, preferred_element_type=F32)
    shape = (seqs, seq_len, heads, HEAD_DIM)
    queries = ((projected[0] + bias_q) * scale).astype(BF16).reshape(shape)
    keys = projected[1].astype(BF16).reshape(shape)
    values = (projected[2] + bias_v).astype(BF16).reshape(shape)
    scores = jnp.einsum("sqhd,skhd->shqk", queries, keys, preferred_element_type=F32)
    valid = positions[None, :] < length[:, None]
    scores = jnp.where(valid[:, None, None, :], scores, -1e30)
    expanded = jnp.exp(scores - jnp.max(scores, axis=-1, keepdims=True))
    probs = expanded / jnp.sum(expanded, axis=-1, keepdims=True)
    low_probs = probs.astype(BF16)
    context = jnp.einsum("shqk,skhd->sqhd", low_probs, values, preferred_element_type=F32)
    context = context.reshape(seqs, seq_len, width).astype(BF16)
    attended = jnp.einsum("mqg,ag->mqa", context, wo, preferred_element_type=F32)
    normed, normal_attn, inv_attn = norm_parts(embedded + attended + bias_out, gain_attn, shift_attn)
    inner = jnp.einsum("twv,ve->twe", normed.astype(BF16), wup, preferred_element_type=F32) + expand_bias
    cdf = 0.5 * (1.0 + lax.erf(inner * math.sqrt(0.5)))
    slope = cdf + inner * jnp.exp(-0.5 * inner * inner) * (1.0 / math.sqrt(2.0 * math.pi))
    active = (inner * cdf).astype(BF16)
    ffn_out = jnp.einsum("jrx,vx->jrv", active, wdown, preferred_element_type=F32)
    result, normal_ffn, inv_ffn = norm_parts(normed + ffn_out + bias_down, gain_ffn, shift_ffn)
    out_hidden = to_tokens(result.astype(BF16))
    dy = grad_rows.astype(F32)
    grad_mid = norm_back(dy, normal_ffn, inv_ffn, gain_ffn)
    grad_active = jnp.einsum("twv,ve->twe", grad_mid.astype(BF16), wdown, preferred_element_type=F32)
    grad_inner = (grad_active * slope).astype(BF16)
    grad_normed = grad_mid + jnp.einsum("jrx,vx->jrv", grad_inner, wup, preferred_element_type=F32)
    grad_first = norm_back(grad_normed, normal_attn, inv_attn, gain_attn)
    grad_context = jnp.einsum("fox,xn->fon", grad_first.astype(BF16), wo, preferred_element_type=F32)
    grad_context = grad_context.astype(BF16).reshape(shape)
    grad_probs = jnp.einsum("sqhd,skhd->shqk", grad_context, values, preferred_element_type=F32)
    grad_values = jnp.einsum("shqk,sqhd->skhd", low_probs, grad_context, preferred_element_type=F32).astype(BF16)
    inner_sum = jnp.sum(probs * grad_probs, axis=-1, keepdims=True)
    grad_scores = (probs * (grad_probs - inner_sum)).astype(BF16)
    grad_queries = jnp.einsum("shqk,skhd->sqhd", grad_scores, keys, preferred_element_type=F32).astype(BF16) * scale
    grad_keys = jnp.einsum("shqk,sqhd->skhd", grad_scores, queries, preferred_element_type=F32).astype(BF16)
    flat = (seqs, seq_len, width)
    grad_queries, grad_keys, grad_values = (g.reshape(flat) for g in (grad_queries, grad_keys, grad_values))
    stacked = jnp.stack([grad_queries, grad_keys, grad_values], axis=2)
    grad_embedded = grad_first + jnp.einsum("hgax,bax->hgb", stacked, wqkv, preferred_element_type=F32)
    grad_hidden = to_tokens(grad_embedded.astype(BF16))
    sums = tuple(
        jnp.sum(g.astype(F32), axis=(0, 1)) * (1.0 / total_tokens)
        for g in (grad_queries, grad_values, grad_first, grad_inner, grad_mid, grad_normed, dy)
    )
    return (out_hidden, grad_hidden) + lax.psum(sums, ("dp", "mp"))


def solution(mesh):
    rows = P("dp", "mp", None)
    frozen = P("dp", "mp")
    placed = (rows, P("dp"), P("dp"), P(), P("dp", None, "mp"), frozen, frozen, frozen) + (P(),) * 9 + (rows,)
    return jax.shard_map(on_device, mesh=mesh, in_specs=placed, out_specs=(rows, rows) + (P(),) * 7, check_vma=False)
```

time: 1120 us -> 798 us (0.71)
  waiting for transfers between devices: 796 us -> 473 us
  blocking collectives: 53.7 us -> 114 us
  matrix products: 161 us -> 108 us
  other arithmetic: 62.3 us -> 32.4 us
  local copies, waits for them, and re-layouts: 21.1 us -> 37.9 us
    reduce_scatter x16 -> x0, waiting for transfers between devices: 411 us -> none  [the longest x4 172 us: run_group(): lax.psum_scatter(attn_terms, 'mp', scatter_dimension=1, tiled=True)]
    dot_general x56 -> x13, matrix products: 161 us -> 96.3 us  [the longest x1 12.5 us: on_device(): jnp.einsum('twv,ve->twe', grad_mid.astype(BF16), wdown, preferred_element...]
    all_to_all x0 -> x3, waiting for transfers between devices: none -> 58.2 us  [the longest x1 46.4 us: to_sequences(): return lax.all_to_all(rows, 'mp', split_axis=0, concat_axis=1, tiled=True)]
    all_to_all x0 -> x1, blocking collectives: none -> 56.9 us  [to_sequences(): return lax.all_to_all(rows, 'mp', split_axis=0, concat_axis=1, tiled=True)]
    all_gather x19 -> x7, waiting for transfers between devices: 378 us -> 413 us  [the longest x4 335 us: gather_whole(): return lax.all_gather(rows, 'mp', axis=rows.ndim - 1, tiled=True)]
    reduce_sum x20 -> x6, other arithmetic: 22.9 us -> 4.73 us  [the longest x3 3.47 us: on_device(): jnp.sum(g.astype(F32), axis=(0, 1)) * (1.0 / total_tokens)]
    convert_element_type x18 -> x2, other arithmetic: 29 us -> 12.4 us  [the longest x1 11.8 us: on_device(): grad_scores = (probs * (grad_probs - inner_sum)).astype(BF16)]
    unnamed x2 -> x3, other arithmetic: 0.15 us -> 14.5 us
  transfers between devices with their start and end apart: 35 -> 10, of which waited for: 33 -> 9; matrix products, arithmetic and copies ran while one was open for 19% -> 9% of each run, Pallas kernels for 0% -> 0%
where the time goes in v1:
time: 798 us; the launch traced here: 791 us
  waiting for transfers between devices  473 us (59%)
  blocking collectives  114 us (14%)
  matrix products  108 us (14%)
  local copies, waits for them, and re-layouts  37.9 us (5%)
  other arithmetic  32.4 us (4%)
  between operations  14.8 us (2%)
  starting transfers between devices  11.8 us (1%)
    all_gather x4, waiting for transfers between devices, gather_whole(): return lax.all_gather(rows, 'mp', axis=rows.ndim - 1, tiled=True)  335 us
    all_gather x3, waiting for transfers between devices, gather_whole(): rows = lax.all_gather(shard, 'dp', axis=0, tiled=True)  77.2 us
    all_to_all x1, blocking collectives, to_sequences(): return lax.all_to_all(rows, 'mp', split_axis=0, concat_axis=1, tiled=True)  56.9 us
    all_to_all x1, waiting for transfers between devices, to_sequences(): return lax.all_to_all(rows, 'mp', split_axis=0, concat_axis=1, tiled=True)  46.4 us
    psum x1, blocking collectives, on_device(): return (out_hidden, grad_hidden) + lax.psum(sums, ('dp', 'mp'))  46.1 us
    unnamed x59, local copies, waits for them, and re-layouts  16 us
  transfers between devices with their start and end apart: 10, of which 9 were waited for; matrix products, arithmetic and copies ran while one was open for 9% of the time, Pallas kernels for 0%

profile of v1, /device:TPU:0, one launch (start us, length us, event | category | flops | bytes accessed | tf_op | source)
XLA Modules:
  0.0 791.5 jit_solution(3417664320677252140)
XLA Ops:
  9.4 28.8 %all-gather.8.cloned.1.call-done = bf16[1024,3,256]{2,0,1:T(8,128)(2,1)} async-done(((bf16[128,3,256]{2,0,1:T(8,128)(2,1)}), bf16[1024,3,256]{2,0,1:T(8,128)(2,1)}) %all-gather.8.cloned.1.call-update) | async-done | bytes 1572880 | tf_op jit(solution)/shard_map/all_gather | solution.py:35
  38.3 10.8 %all_gather.26 = bf16[1024,256]{1,0:T(8,128)(2,1)} all-gather(bf16[128,256]{1,0:T(8,128)(2,1)S(1)} %copy-done.9), channel_id=1, replica_groups=mesh['dp'=8,'mp'=4] {'dp'}, dimensions={0}, use_global_device_ids=true | all-gather | bytes 589824 | tf_op jit(solution)/shard_map/all_gather | solution.py:35
  49.2 18.8 %all-gather.14.cloned.1.call-done = bf16[1024,1024]{1,0:T(8,128)(2,1)} async-done(((bf16[128,1024]{1,0:T(8,128)(2,1)}), bf16[1024,1024]{1,0:T(8,128)(2,1)}) %all-gather.14.cloned.1.call-update) | async-done | bytes 2097168 | tf_op jit(solution)/shard_map/all_gather | solution.py:35
  68.0 29.6 %all-gather.18.cloned.1.call-done = bf16[1024,1024]{1,0:T(8,128)(2,1)} async-done(((bf16[128,1024]{1,0:T(8,128)(2,1)}), bf16[1024,1024]{1,0:T(8,128)(2,1)}) %all-gather.18.cloned.1.call-update) | async-done | bytes 2097168 | tf_op jit(solution)/shard_map/all_gather | solution.py:35
  97.7 56.9 %all_to_all.42 = bf16[4,128,1024]{2,1,0:T(8,128)(2,1)S(1)} all-to-all(bf16[4,128,1024]{2,1,0:T(8,128)(2,1)S(1)} %copy-done.6), channel_id=1, replica_groups=mesh['dp'=8,'mp'=4] {'mp'}, dimensions={0} | all-to-all | bytes 2097152 | tf_op jit(solution)/shard_map/all_to_all | solution.py:48
  161.8 46.4 %all-to-all-done = bf16[4,128,1024]{2,1,0:T(8,128)(2,1)S(1)} async-done(((bf16[4,128,1024]{2,1,0:T(8,128)(2,1)}), bf16[4,128,1024]{2,1,0:T(8,128)(2,1)S(1)}, u32[]{:S(2)}, u32[]{:S(2)}) %all-to-all-start) | async-done | bytes 1048608 | tf_op jit(solution)/shard_map/all_to_all | solution.py:48
  208.2 44.6 %all-gather.10.cloned.1.call-done = bf16[1024,3,1024]{2,0,1:T(8,128)(2,1)} async-done(((bf16[1024,3,256]{2,0,1:T(8,128)(2,1)}), bf16[1024,3,1024]{2,0,1:T(8,128)(2,1)}) %all-gather.10.cloned.1.call-update) | async-done | bytes 6291472 | tf_op jit(solution)/shard_map/all_gather | solution.py:36
  269.2 11.7 %fusion.59 = (f32[16,512]{1,0:T(8,128)S(1)}, f32[16,512,512]{1,2,0:T(8,128)}) fusion(pred[512]{0:T(512)(128)(4,1)S(1)} %iota_compare_fusion, bf16[512,16,64]{0,2,1:T(8,128)(2,1)} %bitcast.100, f32[512,16,64]{0,2,1:T(8,128)S(1)} %bitcast.94, f32[16,64]{1,0:T(8,128)S(1)} %add.163), kind=kOutput, calls=%fused_computation.105 | convolution fusion | flops 551027200 | bytes 19960320 | tf_op jit(solution)/shard_map/sub | solution.py:75
  280.9 9.1 %fusion.29 = bf16[16,64,512]{2,1,0:T(8,128)(2,1)} fusion(f32[512,16,64]{0,2,1:T(8,128)} %bitcast.104, f32[16,64]{1,0:T(8,128)S(1)} %add.160, f32[16,512,512]{1,2,0:T(8,128)} %get-tuple-element.31, f32[16,512]{1,0:T(8,128)S(1)} %get-tuple-element.30), kind=kOutput, calls=%fused_computation.64 | convolution fusion | flops 546832384 | bytes 19959808 | tf_op jit(solution)/shard_map/shqk,skhd->sqhd/dot_general | solution.py:78
  289.9 9.9 %all-gather.12.cloned.1.call-done = bf16[1024,1024]{1,0:T(8,128)(2,1)} async-done(((bf16[1024,256]{1,0:T(8,128)(2,1)}), bf16[1024,1024]{1,0:T(8,128)(2,1)}) %all-gather.12.cloned.1.call-update) | async-done | bytes 2097168 | tf_op jit(solution)/shard_map/all_gather | solution.py:36
  305.5 143.7 %all-gather.16.cloned.1.call-done = bf16[1024,4096]{1,0:T(8,128)(2,1)} async-done(((bf16[1024,1024]{1,0:T(8,128)(2,1)}), bf16[1024,4096]{1,0:T(8,128)(2,1)}) %all-gather.16.cloned.1.call-update) | async-done | bytes 8388624 | tf_op jit(solution)/shard_map/all_gather | solution.py:36
  449.1 12.2 %fusion.37 = f32[512,4096]{1,0:T(8,128)} fusion(bf16[1024,4096]{1,0:T(8,128)(2,1)} %all-gather.16.cloned.1.call-done, f32[512,1024]{1,0:T(8,128)} %copy-done, f32[1024]{0:T(1024)S(1)} %copy-done.21, f32[1024]{0:T(1024)S(1)} %copy-done.13, f32[512]{0:T(512)S(1)} %add_rsqrt_fusion.1, f32[512]{0:T(512)S(1)} %broadcast_multiply_fusion.11), kind=kOutput, calls=%fused_computation.68 | convolution fusion | flops 4297588736 | bytes 18886656 | tf_op jit(solution)/shard_map/twv,ve->twe/dot_general | solution.py:82
  461.4 137.2 %all-gather.20.cloned.1.call-done = bf16[1024,4096]{1,0:T(8,128)(2,1)} async-done(((bf16[1024,1024]{1,0:T(8,128)(2,1)}), bf16[1024,4096]{1,0:T(8,128)(2,1)}) %all-gather.20.cloned.1.call-update) | async-done | bytes 8388624 | tf_op jit(solution)/shard_map/all_gather | solution.py:36
  598.5 10.2 %fusion.61 = (f32[512]{0:T(512)S(1)}, f32[512,1024]{1,0:T(8,128)S(1)}) fusion(f32[1024]{0:T(1024)S(1)} %copy-done.20, bf16[1024,4096]{1,0:T(8,128)(2,1)} %all-gather.20.cloned.1.call-done, f32[512,4096]{1,0:T(8,128)} %fusion.37, f32[4096]{0:T(1024)S(1)} %copy-done.18, f32[1024]{0:T(1024)S(1)} %copy-done.21, f32[1024]{0:T(1024)S(1)} %copy-done.13, ...), kind=kOutput, calls=%fused_computation.107 | convolution fusion | flops 4311219712 | bytes 21006336 | tf_op jit(solution)/shard_map/jrx,vx->jrv/dot_general | solution.py:86
  611.6 12.5 %convert_reduce_fusion = (f32[4096]{0:T(1024)S(1)}, bf16[512,4096]{1,0:T(8,128)(2,1)}) fusion(f32[512,4096]{1,0:T(8,128)} %fusion.37, f32[4096]{0:T(1024)S(1)} %copy-done.18, bf16[1024,4096]{1,0:T(8,128)(2,1)} %all-gather.20.cloned.1.call-done, f32[512,1024]{1,0:T(8,128)S(1)} %get-tuple-element.22), kind=kOutput, calls=%fused_computation.13 | convolution fusion | flops 4322750464 | bytes 23101440 | tf_op jit(solution)/shard_map/twv,ve->twe/dot_general | solution.py:91
  624.2 7.0 multiply_reduce_fusion.6
  637.0 11.6 %multiply_reduce_fusion = (f32[16,512]{1,0:T(8,128)S(1)}, f32[16,512,512]{1,2,0:T(8,128)}) fusion(f32[16,512,512]{1,2,0:T(8,128)} %get-tuple-element.31, f32[16,512]{1,0:T(8,128)S(1)} %get-tuple-element.30, bf16[512,16,64]{0,2,1:T(8,128)(2,1)S(1)} %bitcast.111, f32[512,16,64]{0,2,1:T(8,128)} %bitcast.105, f32[16,64]{1,0:T(8,128)S(1)} %add.160), kind=kOutput, calls=%fused_computation.2 | convolution fusion | flops 550494208 | bytes 36769792 | tf_op jit(solution)/shard_map/sqhd,skhd->shqk/dot_general | solution.py:97
  648.6 9.4 %convert_reduce_fusion.1 = (f32[16,64]{1,0:T(8,128)S(1)}, bf16[16,64,512]{2,1,0:T(8,128)(2,1)}) fusion(bf16[512,16,64]{0,2,1:T(8,128)(2,1)S(1)} %bitcast.112, f32[16,512,512]{1,2,0:T(8,128)} %get-tuple-element.31, f32[16,512]{1,0:T(8,128)S(1)} %get-tuple-element.30), kind=kOutput, calls=%fused_computation.38 | convolution fusion | flops 546831360 | bytes 18911232 | tf_op jit(solution)/shard_map/shqk,sqhd->skhd/dot_general | solution.py:98
  658.0 11.8 %multiply_convert_fusion = bf16[16,512,512]{1,2,0:T(8,128)(2,1)S(1)} fusion(f32[16,512,512]{1,2,0:T(8,128)} %get-tuple-element.38, f32[16,512]{1,0:T(8,128)S(1)} %get-tuple-element.37, f32[16,512,512]{1,2,0:T(8,128)} %get-tuple-element.31, f32[16,512]{1,0:T(8,128)S(1)} %get-tuple-element.30), kind=kLoop, calls=%fused_computation.1 | loop fusion | flops 16777216 | bytes 42008576 | tf_op jit(solution)/shard_map/convert_element_type | solution.py:100
  679.6 7.2 fusion.35
  689.0 6.8 reduce.38
  704.3 7.8 reduce.37
  715.8 11.8 %all-to-all-done.3 = bf16[4,2,65536]{2,1,0:T(2,128)(2,1)S(1)} async-done(((bf16[4,2,65536]{2,1,0:T(2,128)(2,1)}), bf16[4,2,65536]{2,1,0:T(2,128)(2,1)S(1)}, u32[]{:S(2)}, u32[]{:S(2)}) %all-to-all-start.3) | async-done | bytes 1048608 | tf_op jit(solution)/shard_map/all_to_all | solution.py:51
  732.0 46.1 %all-reduce = (f32[1024]{0:T(1024)}, f32[1024]{0:T(1024)}, f32[1024]{0:T(1024)}, f32[4096]{0:T(1024)}, f32[1024]{0:T(1024)}, /*index=5*/f32[1024]{0:T(1024)}, f32[1024]{0:T(1024)}) all-reduce(f32[1024]{0:T(1024)S(1)} %mul.272, f32[1024]{0:T(1024)S(1)} %mul.274, ...), channel_id=1, replica_groups=mesh['dp'=8,'mp'=4] {'dp','mp'}, use_global_device_ids=true, to_apply=%region_12.13 | all-reduce | flops 10240 | bytes 81920 | tf_op jit(solution)/shard_map/psum | solution.py:112
  (123 shorter events, 74.9 us)
Async XLA Ops:
  7.2 31.1 %copy-start.9 = (bf16[128,256]{1,0:T(8,128)(2,1)S(1)}, bf16[128,256]{1,0:T(8,128)(2,1)}, u32[]{:S(2)}) copy-start(bf16[128,256]{1,0:T(8,128)(2,1)} %param.23) | copy-start | bytes 196612
  7.2 31.0 %all-gather.8.cloned.1.call-start = ((), (), s32[]{:S(2)}) async-start(), calls=%async_computation.4 | async-start | bytes 1769472 | tf_op jit(solution)/shard_map/all_gather | solution.py:35
  7.9 60.0 %all-gather.14.cloned.1.call-start = ((), (), s32[]{:S(2)}) async-start(), calls=%async_computation.7 | async-start | bytes 2359296 | tf_op jit(solution)/shard_map/all_gather | solution.py:35
  8.7 89.0 %all-gather.18.cloned.1.call-start = ((), (), s32[]{:S(2)}) async-start(), calls=%async_computation.9 | async-start | bytes 2359296 | tf_op jit(solution)/shard_map/all_gather | solution.py:35
  9.4 243.5 %all-gather.10.cloned.1.call-start = ((), (), s32[]{:S(2)}) async-start(), calls=%async_computation.5 | async-start | bytes 7864320 | tf_op jit(solution)/shard_map/all_gather | solution.py:36
  38.3 261.6 %all-gather.12.cloned.1.call-start = ((), (), s32[]{:S(2)}) async-start(), calls=%async_computation.6 | async-start | bytes 2621440 | tf_op jit(solution)/shard_map/all_gather | solution.py:36
  49.1 400.0 %all-gather.16.cloned.1.call-start = ((), (), s32[]{:S(2)}) async-start(), calls=%async_computation.8 | async-start | bytes 10485760 | tf_op jit(solution)/shard_map/all_gather | solution.py:36
  67.9 29.7 %copy-start.6 = (bf16[4,128,1024]{2,1,0:T(8,128)(2,1)S(1)}, bf16[4,128,1024]{2,1,0:T(8,128)(2,1)}, u32[]{:S(2)}) copy-start(bf16[4,128,1024]{2,1,0:T(8,128)(2,1)} %param.35) | copy-start | bytes 3145732
  67.9 530.6 %all-gather.20.cloned.1.call-start = ((), (), s32[]{:S(2)}) async-start(), calls=%async_computation.10 | async-start | bytes 10485760 | tf_op jit(solution)/shard_map/all_gather | solution.py:36
  97.7 60.6 %copy-start.22 = (s32[4]{0:T(128)S(1)}, s32[4]{0:T(128)}, u32[]{:S(2)}) copy-start(s32[4]{0:T(128)} %param.20) | copy-start | bytes 52
  97.7 61.1 %copy-start.23 = (s32[4]{0:T(128)S(1)}, s32[4]{0:T(128)}, u32[]{:S(2)}) copy-start(s32[4]{0:T(128)} %param.19) | copy-start | bytes 52
  97.7 61.7 %copy-start.14 = (f32[1024]{0:T(1024)S(1)}, f32[1024]{0:T(1024)}, u32[]{:S(2)}) copy-start(f32[1024]{0:T(1024)} %param.26) | copy-start | bytes 12292
  97.7 61.8 %copy-start.15 = (f32[1024]{0:T(1024)S(1)}, f32[1024]{0:T(1024)}, u32[]{:S(2)}) copy-start(f32[1024]{0:T(1024)} %param.27) | copy-start | bytes 12292
  97.7 61.8 %copy-start.12 = (f32[2,1024]{1,0:T(2,128)S(1)}, f32[2,1024]{1,0:T(2,128)}, u32[]{:S(2)}) copy-start(f32[2,1024]{1,0:T(2,128)} %param.21) | copy-start | bytes 24580
  97.7 63.2 %copy-start.10 = (f32[1024]{0:T(1024)S(1)}, f32[1024]{0:T(1024)}, u32[]{:S(2)}) copy-start(f32[1024]{0:T(1024)} %param.33) | copy-start | bytes 12292
  154.7 53.6 %all-to-all-start = ((bf16[4,128,1024]{2,1,0:T(8,128)(2,1)}), bf16[4,128,1024]{2,1,0:T(8,128)(2,1)S(1)}, u32[]{:S(2)}, u32[]{:S(2)}) async-start(bf16[4,128,1024]{2,1,0:T(8,128)(2,1)} %param.18), calls=%async_computation | async-start | bytes 2097152 | tf_op jit(solution)/shard_map/all_to_all | solution.py:48
  208.2 50.3 %copy-start.7 = (bf16[4,128,1024]{2,1,0:T(8,128)(2,1)}, bf16[4,128,1024]{2,1,0:T(8,128)(2,1)S(1)}, u32[]{:S(2)}) copy-start(bf16[4,128,1024]{2,1,0:T(8,128)(2,1)S(1)} %all-to-all-done) | copy-start | bytes 3145732
  303.8 145.3 %copy-start.13 = (f32[1024]{0:T(1024)S(1)}, f32[1024]{0:T(1024)}, u32[]{:S(2)}) copy-start(f32[1024]{0:T(1024)} %param.31) | copy-start | bytes 12292
  303.8 145.3 %copy-start.21 = (f32[1024]{0:T(1024)S(1)}, f32[1024]{0:T(1024)}, u32[]{:S(2)}) copy-start(f32[1024]{0:T(1024)} %param.32) | copy-start | bytes 12292
  305.4 293.1 %copy-start.18 = (f32[4096]{0:T(1024)S(1)}, f32[4096]{0:T(1024)}, u32[]{:S(2)}) copy-start(f32[4096]{0:T(1024)} %param.29) | copy-start | bytes 49156
  305.4 293.1 %copy-start.20 = (f32[1024]{0:T(1024)S(1)}, f32[1024]{0:T(1024)}, u32[]{:S(2)}) copy-start(f32[1024]{0:T(1024)} %param.30) | copy-start | bytes 12292
  697.8 29.9 %all-to-all-start.3 = ((bf16[4,2,65536]{2,1,0:T(2,128)(2,1)}), bf16[4,2,65536]{2,1,0:T(2,128)(2,1)S(1)}, u32[]{:S(2)}, u32[]{:S(2)}) async-start(bf16[4,2,65536]{2,1,0:T(2,128)(2,1)} %reshape.461), calls=%async_computation.3 | async-start | bytes 2097152 | tf_op jit(solution)/shard_map/all_to_all | solution.py:51
  712.1 19.9 %copy-start.11 = (f32[1024]{0:T(1024)S(1)}, f32[1024]{0:T(1024)}, u32[]{:S(2)}) copy-start(f32[1024]{0:T(1024)} %get-tuple-element.12) | copy-start | bytes 12292
  727.6 52.8 %all-to-all-start.1 = ((bf16[4,2,65536]{2,1,0:T(2,128)(2,1)}), bf16[4,2,65536]{2,1,0:T(2,128)(2,1)}, u32[]{:S(2)}, u32[]{:S(2)}) async-start(bf16[4,2,65536]{2,1,0:T(2,128)(2,1)} %reshape.459), calls=%async_computation.1 | async-start | bytes 2097152 | tf_op jit(solution)/shard_map/all_to_all | solution.py:51
  (12 other events, 81.5 us)
Sparse Core Ops, SparseCore 0:
  9.9 28.2 all-gather.7
  40.1 27.7 all-gather.13
  69.8 27.7 all-gather.17
  99.0 153.8 all-gather.9
  254.3 45.5 all-gather.11
  301.3 147.7 all-gather.15
  450.7 147.7 all-gather.19

commit v2 on v1

v2 whole, which is shorter than its diff:
```python
import functools
import math

import jax
import jax.numpy as jnp
from jax import lax
from jax.experimental import pallas as pl
from jax.experimental.pallas import tpu as pltpu
from jax.sharding import PartitionSpec as P

HEAD_DIM = 64
EPS = 1e-12
F32 = jnp.float32
BF16 = jnp.bfloat16
MESH = pl.DeviceIdType.MESH
ROWS = 64
NN = ((1,), (0,))
NT = ((1,), (1,))


def dot(a, b, dims=NN):
    return lax.dot_general(a, b, (dims, ((), ())), preferred_element_type=F32)


def snake(pos):
    high = pos // 2
    return 2 * high + (pos % 2 + high) % 2


def row_mean(x):
    return jnp.sum(x, axis=-1, keepdims=True) * (1.0 / x.shape[-1])


def step_kernel(
    shape, lens, seps, seg, bias_q, bias_v, bias_out, expand_bias, bias_down, gain_attn, shift_attn, gain_ffn,
    shift_ffn, hid, cot, wq_in, wo_in, wu_in, wd_in,
    out, grad, sum_q, sum_v, sum_out, sum_up, sum_down, sum_attn, sum_ffn,
    wq, wo, wu, wd, xh, ct, outb, low, qs, ks, vs, probs, normal, inverse, acc, act, slope, gctx,
    local_sem, ici_sem, sib_sem, send_sem, row_recv, row_send,
):
    dp, mp, seq, width, units = shape
    ring, half = dp // 2, dp // 4
    rb = width // dp
    cq = width // mp
    cu = units // mp
    hu = cu // 2
    tok = seq // mp
    heads = width // HEAD_DIM
    scale = 1.0 / math.sqrt(HEAD_DIM)
    d = lax.axis_index("dp")
    z = lax.axis_index("mp")
    core = d % 2
    pos = snake(d // 2)
    right = (2 * snake((pos + 1) % ring) + core, z)
    left = (2 * snake((pos + ring - 1) % ring) + core, z)
    sibling = (d + 1 - 2 * core, z)
    wholes = (wq, wo, wu, wd)
    shards = (wq_in, wo_in, wu_in, wd_in)

    def region(b, j, k, origin):
        zz = (z + mp - k) % mp
        rows = pl.ds(pl.multiple_of((2 * snake(origin) + core) * rb, rb), rb)
        if b == 0:
            return wq.at[:, rows, pl.ds(pl.multiple_of(zz * cq, 128), cq)]
        if b == 1:
            return wo.at[rows, pl.ds(pl.multiple_of(zz * cq, 128), cq)]
        return wholes[b].at[rows, pl.ds(pl.multiple_of(zz * cu + j * hu, 128), hu)]

    def own_shard(b, j):
        if b < 2:
            return shards[b]
        return shards[b].at[:, pl.ds(pl.multiple_of(j * hu, 128), hu)]

    def piece(b, j):
        return (0, 1, 2, 4)[b] + j

    def send(src, b, j, k, origin, way, target):
        zz = (z + mp - k) % mp
        dst = region(b, j, k, origin)
        recv = sib_sem.at[piece(b, j), zz] if way == 2 else ici_sem.at[piece(b, j), zz, origin]
        pltpu.make_async_remote_copy(
            src_ref=src, dst_ref=dst, send_sem=send_sem.at[b, way], recv_sem=recv, device_id=target, device_id_type=MESH
        ).start()

    def arrived(b, j, k, origin):
        zz = (z + mp - k) % mp
        ref = region(b, j, k, origin)
        pltpu.make_async_copy(ref, ref, ici_sem.at[piece(b, j), zz, origin]).wait()
        return ref

    def spread(src, b, j, k):
        send(src, b, j, k, pos, 0, right)
        send(src, b, j, k, pos, 1, left)
        send(src, b, j, k, pos, 2, sibling)

    def start_own(b, j):
        for hop in range(1, mp):
            there = (z + hop) % mp
            send_z(b, j, there)
        spread(own_shard(b, j), b, j, 0)

    def send_z(b, j, there):
        pltpu.make_async_remote_copy(
            src_ref=own_shard(b, j), dst_ref=region(b, j, 0, pos), send_sem=send_sem.at[b, 3],
            recv_sem=ici_sem.at[piece(b, j), z, pos], device_id=(d, there), device_id_type=MESH,
        ).start()

    def serve_column(b, j, k):
        spread(arrived(b, j, k, pos), b, j, k)

    def pick(cond, fn):
        if isinstance(cond, bool):
            if cond:
                fn()
        else:
            pl.when(cond)(fn)

    def serve_ring(b, j, k, dist):
        even, odd = k % 2 == 0, k % 2 == 1

        def from_left():
            origin = (pos + ring - dist) % ring
            ref = arrived(b, j, k, origin)
            if dist + 1 < half:
                send(ref, b, j, k, origin, 0, right)
            elif dist + 1 == half:
                pick(even, lambda: send(ref, b, j, k, origin, 0, right))
            send(ref, b, j, k, origin, 2, sibling)

        def from_right():
            origin = (pos + dist) % ring
            ref = arrived(b, j, k, origin)
            if dist + 1 < half:
                send(ref, b, j, k, origin, 1, left)
            elif dist + 1 == half:
                pick(odd, lambda: send(ref, b, j, k, origin, 1, left))
            send(ref, b, j, k, origin, 2, sibling)

        if dist < half:
            from_left()
            from_right()
        else:
            pick(even, from_left)
            pick(odd, from_right)

    def serve_item(b, j, k):
        pick(k > 0, lambda: serve_column(b, j, k))
        for dist in range(1, half + 1):
            serve_ring(b, j, k, dist)

    def sibling_done(b, j, k):
        zz = (z + mp - k) % mp
        if b == 0:
            ref = wq.at[:, pl.ds(0, width // 2), pl.ds(0, cq)]
        elif b == 1:
            ref = wo.at[pl.ds(0, width // 2), pl.ds(0, cq)]
        else:
            ref = wholes[b].at[pl.ds(0, width // 2), pl.ds(0, hu)]
        pltpu.make_async_copy(ref, ref, sib_sem.at[piece(b, j), zz]).wait()

    def tokens(ref, block):
        return ref.at[pl.ds(pl.multiple_of(block * tok, tok), tok), :]

    def own_local(b):
        zz = z
        rows = pl.ds(pl.multiple_of(d * rb, rb), rb)
        if b == 0:
            dst = wq.at[:, rows, pl.ds(pl.multiple_of(zz * cq, 128), cq)]
        elif b == 1:
            dst = wo.at[rows, pl.ds(pl.multiple_of(zz * cq, 128), cq)]
        else:
            dst = wholes[b].at[rows, pl.ds(pl.multiple_of(zz * cu, 128), cu)]
        return pltpu.make_async_copy(shards[b], dst, local_sem.at[b])

    barrier = pltpu.get_barrier_semaphore()
    partners = [sibling, right, left] + [(d, (z + hop) % mp) for hop in range(1, mp)]
    for target in partners:
        pl.semaphore_signal(barrier, inc=1, device_id=target, device_id_type=MESH)
    for b in range(4):
        own_local(b).start()
    own_hid = pltpu.make_async_copy(hid.at[z], tokens(xh, z), local_sem.at[4])
    own_cot = pltpu.make_async_copy(cot.at[z], tokens(ct, z), local_sem.at[5])
    own_hid.start()
    own_cot.start()
    pl.semaphore_wait(barrier, len(partners))

    def exchange_in(src, dst, which):
        for hop in range(1, mp):
            there = (z + hop) % mp
            pltpu.make_async_remote_copy(
                src_ref=src.at[there], dst_ref=tokens(dst, z), send_sem=row_send.at[which, there],
                recv_sem=row_recv.at[which, z], device_id=(d, there), device_id_type=MESH,
            ).start()

    def exchange_wait(src, dst, which):
        for hop in range(1, mp):
            there = (z + hop) % mp
            pltpu.make_async_copy(tokens(dst, there), tokens(dst, there), row_recv.at[which, there]).wait()

    def sends_wait(ref, which):
        for hop in range(1, mp):
            there = (z + hop) % mp
            pltpu.make_async_copy(ref, ref, row_send.at[which, there]).wait()

    start_own(0, 0)
    exchange_in(hid, xh, 0)
    start_own(1, 0)
    for b in (2, 3):
        for j in range(2):
            start_own(b, j)
    exchange_in(cot, ct, 1)

    for b in range(2):
        for k in range(mp):
            serve_item(b, 0, k)
    own_hid.wait()
    exchange_wait(hid, xh, 0)
    length = lens[z]
    separator = seps[z]
    seg0 = seg[0:1, :]
    seg_step = seg[1:2, :] - seg[0:1, :]

    def embed(rows, first):
        at = lax.broadcasted_iota(jnp.int32, (ROWS, 1), 0) + first
        flag = jnp.where(at > separator, 1.0, 0.0).astype(F32)
        return xh[rows, :].astype(F32) + seg0 + flag * seg_step

    @pl.loop(0, seq // ROWS)
    def _(i):
        first = pl.multiple_of(i * ROWS, ROWS)
        rows = pl.ds(first, ROWS)
        low[rows, :] = embed(rows, first).astype(BF16)

    own_local(0).wait()
    for k in range(mp):
        sibling_done(0, 0, k)

    tile = 256

    @pl.loop(0, width // tile)
    def _(i):
        cols = pl.ds(pl.multiple_of(i * tile, tile), tile)
        qs[:, cols] = ((dot(low[...], wq[0, :, cols]) + bias_q[:, cols]) * scale).astype(BF16)
        ks[:, cols] = dot(low[...], wq[1, :, cols]).astype(BF16)
        vs[:, cols] = (dot(low[...], wq[2, :, cols]) + bias_v[:, cols]).astype(BF16)

    pairs = heads // 2
    lane = lax.broadcasted_iota(jnp.int32, (seq, 2 * HEAD_DIM), 1)

    def half_of(x, hh):
        keep = lane < HEAD_DIM if hh == 0 else lane >= HEAD_DIM
        return jnp.where(keep, x, jnp.zeros_like(x))

    items = 2 * mp

    @pl.loop(0, pairs)
    def _(i):
        for part in range(max(1, items // pairs)):
            item = i * max(1, items // pairs) + part
            serve_item(2, item // mp, item % mp)
        cols = pl.ds(pl.multiple_of(i * 128, 128), 128)
        q2 = qs[:, cols]
        k2 = ks[:, cols]
        v2t = vs[:, cols].T
        ctxs = []
        for hh in range(2):
            st = dot(half_of(k2, hh), q2, NT)
            valid = lax.broadcasted_iota(jnp.int32, st.shape, 0) < length
            st = jnp.where(valid, st, -1e30)
            e = jnp.exp(st - jnp.max(st, axis=0, keepdims=True))
            p = (e * (1.0 / jnp.sum(e, axis=0, keepdims=True))).astype(BF16)
            probs[2 * i + hh] = p
            ctxs.append(dot(v2t[hh * HEAD_DIM:(hh + 1) * HEAD_DIM], p))
        low[:, cols] = jnp.concatenate(ctxs, axis=0).T.astype(BF16)

    own_local(1).wait()
    for k in range(mp):
        sibling_done(1, 0, k)

    @pl.loop(0, width // tile)
    def _(i):
        cols = pl.ds(pl.multiple_of(i * tile, tile), tile)
        acc[:, cols] = dot(low[...], wo[cols, :], NT)

    @pl.loop(0, seq // ROWS)
    def _(i):
        first = pl.multiple_of(i * ROWS, ROWS)
        rows = pl.ds(first, ROWS)
        x = embed(rows, first) + acc[rows, :] + bias_out[...]
        center = x - row_mean(x)
        inv = lax.rsqrt(row_mean(center * center) + EPS)
        norm = center * inv
        normal[rows, :] = norm
        inverse[rows, :] = jnp.broadcast_to(inv, (ROWS, 128))
        low[rows, :] = (norm * gain_attn[...] + shift_attn[...]).astype(BF16)
        acc[rows, :] = jnp.zeros((ROWS, width), F32)

    own_local(2).wait()
    for j in range(2):
        for k in range(mp):
            sibling_done(2, j, k)

    tiles = units // tile
    early = mp

    @pl.loop(0, tiles)
    def _(i):
        @pl.when(i % (tiles // early) == 0)
        def _():
            item = i // (tiles // early)
            serve_item(3, item // mp, item % mp)

        cols = pl.ds(pl.multiple_of(i * tile, tile), tile)
        inner = dot(low[...], wu[:, cols]) + expand_bias[:, cols]
        cdf = 0.5 * (1.0 + lax.erf(inner * math.sqrt(0.5)))
        act[:, cols] = (inner * cdf).astype(BF16)
        slope[:, cols] = (cdf + inner * (jnp.exp(-0.5 * inner * inner) * (1.0 / math.sqrt(2.0 * math.pi)))).astype(BF16)

    own_local(3).wait()

    @pl.loop(0, items)
    def _(i):
        @pl.when(i + early < items)
        def _():
            ahead = i + early
            serve_item(3, ahead // mp, ahead % mp)

        j = i // mp
        k = i % mp
        sibling_done(3, j, k)
        zz = (z + mp - k) % mp
        cols = pl.ds(pl.multiple_of(zz * cu + j * hu, 128), hu)

        @pl.loop(0, width // 512)
        def _(n):
            rows = pl.ds(pl.multiple_of(n * 512, 512), 512)
            acc[:, rows] += dot(act[:, cols], wd[rows, cols], NT)

    own_cot.wait()
    exchange_wait(cot, ct, 1)
    sum_ffn[...] = jnp.zeros_like(sum_ffn)
    sum_down[...] = jnp.zeros_like(sum_down)
    sum_attn[...] = jnp.zeros_like(sum_attn)
    sum_out[...] = jnp.zeros_like(sum_out)

    @pl.loop(0, seq // ROWS)
    def _(i):
        rows = pl.ds(pl.multiple_of(i * ROWS, ROWS), ROWS)
        x = normal[rows, :] * gain_attn[...] + shift_attn[...] + acc[rows, :] + bias_down[...]
        center = x - row_mean(x)
        inv = lax.rsqrt(row_mean(center * center) + EPS)
        norm = center * inv
        outb[rows, :] = (norm * gain_ffn[...] + shift_ffn[...]).astype(BF16)
        dy = ct[rows, :].astype(F32)
        e = dy * gain_ffn[...]
        g = inv * (e - row_mean(e) - norm * row_mean(e * norm))
        acc[rows, :] = g
        low[rows, :] = g.astype(BF16)
        sum_ffn[...] += jnp.sum(dy, axis=0, keepdims=True)
        sum_down[...] += jnp.sum(g, axis=0, keepdims=True)

    def push_out(buf, dst, which, there):
        pltpu.make_async_remote_copy(
            src_ref=tokens(buf, there), dst_ref=dst.at[z], send_sem=row_send.at[which, there],
            recv_sem=row_recv.at[which, z], device_id=(d, there), device_id_type=MESH,
        ).start()

    for hop in range(1, mp):
        push_out(outb, out, 2, (z + hop) % mp)
    keep_out = pltpu.make_async_copy(tokens(outb, z), out.at[z], local_sem.at[6])
    keep_out.start()

    @pl.loop(0, tiles)
    def _(i):
        cols = pl.ds(pl.multiple_of(i * tile, tile), tile)
        g = (dot(low[...], wd[:, cols]) * slope[:, cols].astype(F32)).astype(BF16)
        act[:, cols] = g
        sum_up[:, cols] = jnp.sum(g.astype(F32), axis=0, keepdims=True)

    @pl.loop(0, width // tile)
    def _(i):
        cols = pl.ds(pl.multiple_of(i * tile, tile), tile)
        acc[:, cols] += dot(act[...], wu[cols, :], NT)

    @pl.loop(0, seq // ROWS)
    def _(i):
        rows = pl.ds(pl.multiple_of(i * ROWS, ROWS), ROWS)
        g = acc[rows, :]
        norm = normal[rows, :]
        e = g * gain_attn[...]
        first = inverse[rows, 0:1] * (e - row_mean(e) - norm * row_mean(e * norm))
        acc[rows, :] = first
        low[rows, :] = first.astype(BF16)
        sum_attn[...] += jnp.sum(g, axis=0, keepdims=True)
        sum_out[...] += jnp.sum(first, axis=0, keepdims=True)

    @pl.loop(0, width // tile)
    def _(i):
        cols = pl.ds(pl.multiple_of(i * tile, tile), tile)
        gctx[:, cols] = dot(low[...], wo[:, cols]).astype(BF16)

    @pl.loop(0, pairs)
    def _(i):
        cols = pl.ds(pl.multiple_of(i * 128, 128), 128)
        q2 = qs[:, cols]
        k2t = ks[:, cols].T
        v2 = vs[:, cols]
        g2 = gctx[:, cols]
        dq, dk, dv = [], [], []
        for hh in range(2):
            p = probs[2 * i + hh]
            pf = p.astype(F32)
            dpt = dot(half_of(v2, hh), g2, NT)
            ds = (pf * (dpt - jnp.sum(pf * dpt, axis=0, keepdims=True))).astype(BF16)
            dk.append(dot(ds, q2))
            dv.append(dot(p, g2))
            dq.append(dot(k2t[hh * HEAD_DIM:(hh + 1) * HEAD_DIM], ds))
        dq2 = jnp.concatenate(dq, axis=0).T.astype(BF16).astype(F32) * scale
        dv2 = jnp.where(lane < HEAD_DIM, dv[0], dv[1]).astype(BF16)
        qs[:, cols] = dq2.astype(BF16)
        ks[:, cols] = jnp.where(lane < HEAD_DIM, dk[0], dk[1]).astype(BF16)
        vs[:, cols] = dv2
        sum_q[:, cols] = jnp.sum(dq2, axis=0, keepdims=True)
        sum_v[:, cols] = jnp.sum(dv2.astype(F32), axis=0, keepdims=True)

    side = seq // 2
    per = mp // 2
    mine = z // per
    for turn in range(2):
        block = 1 - mine if turn == 0 else mine
        rows = pl.ds(pl.multiple_of(block * side, side), side)

        @pl.loop(0, width // tile)
        def _(i):
            cols = pl.ds(pl.multiple_of(i * tile, tile), tile)
            x = acc[rows, cols]
            x += dot(qs[rows, :], wq[0, cols, :], NT)
            x += dot(ks[rows, :], wq[1, cols, :], NT)
            x += dot(vs[rows, :], wq[2, cols, :], NT)
            xh[rows, cols] = x.astype(BF16)

        for q in range(per):
            there = block * per + (z + q + turn) % per
            if turn == 0 or q < per - 1:
                push_out(xh, grad, 3, there)
    keep_grad = pltpu.make_async_copy(tokens(xh, z), grad.at[z], local_sem.at[7])
    keep_grad.start()

    keep_out.wait()
    keep_grad.wait()
    for which, src in ((0, tokens(xh, z)), (1, tokens(xh, z)), (2, tokens(xh, z)), (3, tokens(xh, z))):
        sends_wait(src, which)
    for which, ref in ((2, out), (3, grad)):
        for hop in range(1, mp):
            there = (z + hop) % mp
            pltpu.make_async_copy(ref.at[there], ref.at[there], row_recv.at[which, there]).wait()
    for b in range(4):
        ref = wholes[b]
        cols = (cq if b < 2 else cu) * mp
        ways = (
            (rb * (2 * half - 1), cols // 2),
            (rb * (2 * half - 1), cols // 2),
            (width // 2, cols),
            (rb, cols - cols // mp),
        )
        for way, (r, c) in enumerate(ways):
            part = ref.at[:, pl.ds(0, r), pl.ds(0, c)] if b == 0 else ref.at[pl.ds(0, r), pl.ds(0, c)]
            pltpu.make_async_copy(part, part, send_sem.at[b, way]).wait()


def on_device(
    hidden_in, lengths, separators, seg_table, query_key_value_weight, output_weight, up_weight, down_weight,
    bias_q, bias_v, bias_out, expand_bias, bias_down, gain_attn, shift_attn, gain_ffn, shift_ffn, cotangent,
):
    dp, mp = lax.axis_size("dp"), lax.axis_size("mp")
    here, tok, width = hidden_in.shape
    assert here == mp
    seq = tok * mp
    units = up_weight.shape[1] * mp
    heads = width // HEAD_DIM
    vmem = pl.BlockSpec(memory_space=pltpu.VMEM)
    smem = pl.BlockSpec(memory_space=pltpu.SMEM)
    anys = pl.BlockSpec(memory_space=pl.ANY)
    rows = [seg_table] + [
        v.reshape(1, -1)
        for v in (bias_q, bias_v, bias_out, expand_bias, bias_down, gain_attn, shift_attn, gain_ffn, shift_ffn)
    ]
    vec = jax.ShapeDtypeStruct((1, width), F32)
    moved = jax.ShapeDtypeStruct(hidden_in.shape, BF16)
    ring = dp // 2
    sem = pltpu.SemaphoreType.DMA
    results = pl.pallas_call(
        functools.partial(step_kernel, (dp, mp, seq, width, units)),
        name="step",
        out_shape=(moved, moved, vec, vec, vec, jax.ShapeDtypeStruct((1, units), F32), vec, vec, vec),
        in_specs=[smem, smem] + [vmem] * 10 + [anys] * 6,
        out_specs=(anys, anys) + (vmem,) * 7,
        scratch_shapes=[
            pltpu.VMEM((3, width, width), BF16),
            pltpu.VMEM((width, width), BF16),
            pltpu.VMEM((width, units), BF16),
            pltpu.VMEM((width, units), BF16),
            *[pltpu.VMEM((seq, width), BF16)] * 7,
            pltpu.VMEM((heads, seq, seq), BF16),
            pltpu.VMEM((seq, width), F32),
            pltpu.VMEM((seq, 128), F32),
            pltpu.VMEM((seq, width), F32),
            pltpu.VMEM((seq, units), BF16),
            pltpu.VMEM((seq, units), BF16),
            pltpu.VMEM((seq, width), BF16),
            sem((8,)),
            sem((6, mp, ring)),
            sem((6, mp)),
            sem((4, 4)),
            sem((4, mp)),
            sem((4, mp)),
        ],
        compiler_params=pltpu.CompilerParams(collective_id=0, has_side_effects=True, vmem_limit_bytes=67043328),
    )(
        lengths, separators, *rows, hidden_in, cotangent, jnp.swapaxes(query_key_value_weight, 0, 1),
        output_weight, up_weight, down_weight,
    )
    factor = 1.0 / (here * seq * dp)
    sums = lax.psum(tuple(s.reshape(-1) for s in results[2:]), ("dp", "mp"))
    return results[:2] + tuple(s * factor for s in sums)


def solution(mesh):
    rows = P("dp", "mp", None)
    frozen = P("dp", "mp")
    placed = (rows, P("dp"), P("dp"), P(), P("dp", None, "mp"), frozen, frozen, frozen) + (P(),) * 9 + (rows,)
    return jax.shard_map(on_device, mesh=mesh, in_specs=placed, out_specs=(rows, rows) + (P(),) * 7, check_vma=False)
```

time: 798 us -> 349 us (0.44)
  waiting for transfers between devices: 473 us -> 0 us
  Pallas kernels: 0 us -> 298 us
  matrix products: 108 us -> 0 us
  blocking collectives: 114 us -> 43.9 us
  local copies, waits for them, and re-layouts: 37.9 us -> 4.02 us
  other arithmetic: 32.4 us -> 2.4 us
  between operations: 14.8 us -> 0.7 us
  starting transfers between devices: 11.8 us -> 0 us
    all_gather x7 -> x0, waiting for transfers between devices: 413 us -> none  [the longest x4 335 us: gather_whole(): return lax.all_gather(rows, 'mp', axis=rows.ndim - 1, tiled=True)]
    pallas_call x0 -> x1, Pallas kernels: none -> 298 us  [on_device(): pl.pallas_call(functools.partial(step_kernel, (dp, mp, seq, width, units)...]
    dot_general x13 -> x0, matrix products: 96.3 us -> none  [the longest x1 12.5 us: on_device(): jnp.einsum('twv,ve->twe', grad_mid.astype(BF16), wdown, preferred_element...]
    all_to_all x3 -> x0, waiting for transfers between devices: 58.2 us -> none  [the longest x1 46.4 us: to_sequences(): return lax.all_to_all(rows, 'mp', split_axis=0, concat_axis=1, tiled=True)]
    all_to_all x1 -> x0, blocking collectives: 56.9 us -> none  [to_sequences(): return lax.all_to_all(rows, 'mp', split_axis=0, concat_axis=1, tiled=True)]
    unnamed x3 -> x0, other arithmetic: 14.5 us -> none
    convert_element_type x2 -> x0, other arithmetic: 12.4 us -> none  [the longest x1 11.8 us: on_device(): grad_scores = (probs * (grad_probs - inner_sum)).astype(BF16)]
    unnamed x59 -> x12, local copies, waits for them, and re-layouts: 16 us -> 4.02 us
  transfers between devices with their start and end apart: 10 -> 0, of which waited for: 9 -> 0; matrix products, arithmetic and copies ran while one was open for 9% -> 0% of each run, Pallas kernels for 0% -> 0%
where the time goes in v2:
time: 349 us
  Pallas kernels  298 us (85%)
  blocking collectives  43.9 us (13%)
  local copies, waits for them, and re-layouts  4.02 us (1%)
    pallas_call x1, Pallas kernels, on_device(): pl.pallas_call(functools.partial(step_kernel, (dp, mp, seq, width, units)...  298 us
    psum x1, blocking collectives, on_device(): sums = lax.psum(tuple((s.reshape(-1) for s in results[2:])), ('dp', 'mp'))  43.9 us

profile of v2, /device:TPU:0, one launch (start us, length us, event | category | flops | bytes accessed | tf_op | source)
XLA Modules:
  0.0 349.0 jit_solution(14020730201596387385)
XLA Ops:
  0.6 297.9 %step.1 = (bf16[4,128,1024]{2,1,0:T(8,128)(2,1)}, bf16[4,128,1024]{2,1,0:T(8,128)(2,1)}, f32[1,1024]{1,0:T(1,128)}, f32[1,1024]{1,0:T(1,128)}, f32[1,1024]{1,0:T...) custom-call(s32[4]{0:T(128)} %lens.1, s32[4]{0:T(128)} %seps.1, ...), custom_call_target="tpu_custom_call" | custom-call | tf_op jit(solution)/shard_map/step/pallas_call | solution.py:492
  298.6 0.0 copy-start.1
  298.6 0.0 copy-start.4
  298.6 0.0 copy-start.3
  298.6 0.0 copy-start.2
  298.6 0.7 copy-done.1
  299.3 0.0 copy-done.4
  299.3 0.0 copy-done.3
  299.3 0.0 copy-done.2
  299.3 43.9 %all-reduce = (f32[1024]{0:T(1024)S(1)}, f32[1024]{0:T(1024)S(1)}, f32[1024]{0:T(1024)S(1)}, f32[4096]{0:T(1024)S(1)}, f32[1024]{0:T(1024)S(1)}, /*index=5*/f32[1024]{0:T(1024)S(1)}, f32[1024]{0:T(1024)S(1)}) all-reduce(f32[1024]{0:T(1024)S(1)} %bitcast.28, f32[1024]{0:T(1024)S(1)} %bitcast.29, ...), channel_id=1, replica_groups=mesh['dp'=8,'mp'=4] {'dp','mp'}, use_global_device_ids=true, to_apply=%region_0.0 | all-reduce | flops 10240 | bytes 81920 | tf_op jit(solution)/shard_map/psum | solution.py:524
  343.2 0.6 broadcast_multiply_fusion.5
  343.8 0.6 broadcast_multiply_fusion.3
  344.4 0.6 broadcast_multiply_fusion.1
  345.0 0.6 broadcast_multiply_fusion
  345.7 0.0 copy-start
  345.7 2.4 copy.29
  348.0 0.0 copy-done
  348.0 1.0 copy.30
Async XLA Ops:
  298.6 0.7 copy-start.1
  298.6 0.7 copy-start.4
  298.6 0.7 copy-start.3
  298.6 0.7 copy-start.2
  345.7 2.4 copy-start

commit v3 on v2

--- a/solution.py
+++ b/solution.py
@@ -14,6 +14,7 @@
 BF16 = jnp.bfloat16
 MESH = pl.DeviceIdType.MESH
 ROWS = 64
+LAG = 0
 NN = ((1,), (0,))
 NT = ((1,), (1,))
 
@@ -34,9 +35,9 @@
 def step_kernel(
     shape, lens, seps, seg, bias_q, bias_v, bias_out, expand_bias, bias_down, gain_attn, shift_attn, gain_ffn,
     shift_ffn, hid, cot, wq_in, wo_in, wu_in, wd_in,
-    out, grad, sum_q, sum_v, sum_out, sum_up, sum_down, sum_attn, sum_ffn,
+    out, grad, sums,
     wq, wo, wu, wd, xh, ct, outb, low, qs, ks, vs, probs, normal, inverse, acc, act, slope, gctx,
-    local_sem, ici_sem, sib_sem, send_sem, row_recv, row_send,
+    early, late, inbox, local_sem, ici_sem, sib_sem, send_sem, row_recv, row_send, sum_recv, sum_send,
 ):
     dp, mp, seq, width, units = shape
     ring, half = dp // 2, dp // 4
@@ -143,10 +144,30 @@
             pick(even, from_left)
             pick(odd, from_right)
 
-    def serve_item(b, j, k):
-        pick(k > 0, lambda: serve_column(b, j, k))
+    total_items = 6 * mp
+    bounds = (0, mp, 2 * mp, 4 * mp, total_items)
+    lag = half + LAG
+
+    def with_item(u, low_u, high_u, fn):
+        if isinstance(u, int):
+            if 0 <= u < total_items:
+                b = sum(u >= x for x in bounds[1:4])
+                fn(b, (u - bounds[b]) // mp, (u - bounds[b]) % mp)
+            return
+        for b in range(4):
+            if low_u < bounds[b + 1] and high_u >= bounds[b]:
+                inside = True
+                if low_u < bounds[b]:
+                    inside = u >= bounds[b]
+                if high_u >= bounds[b + 1]:
+                    inside = (u < bounds[b + 1]) if inside is True else jnp.logical_and(inside, u < bounds[b + 1])
+                pick(inside, lambda b=b: fn(b, (u - bounds[b]) // mp, (u - bounds[b]) % mp))
+
+    def tick(t, low_t=0, high_t=0):
+        with_item(t, low_t, high_t, lambda b, j, k: pick(k > 0, lambda: serve_column(b, j, k)))
         for dist in range(1, half + 1):
-            serve_ring(b, j, k, dist)
+            back = dist + LAG
+            with_item(t - back, low_t - back, high_t - back, lambda b, j, k: serve_ring(b, j, k, dist))
 
     def sibling_done(b, j, k):
         zz = (z + mp - k) % mp
@@ -173,7 +194,12 @@
         return pltpu.make_async_copy(shards[b], dst, local_sem.at[b])
 
     barrier = pltpu.get_barrier_semaphore()
-    partners = [sibling, right, left] + [(d, (z + hop) % mp) for hop in range(1, mp)]
+    def flip(index, bit):
+        return index + bit - 2 * bit * ((index // bit) % 2)
+
+    peers = [(d, flip(z, 1 << s)) for s in range(mp.bit_length() - 1)]
+    peers += [(flip(d, 1 << s), z) for s in range(1, dp.bit_length() - 1)] + [sibling]
+    partners = [sibling, right, left] + [(d, (z + hop) % mp) for hop in range(1, mp)] + peers
     for target in partners:
         pl.semaphore_signal(barrier, inc=1, device_id=target, device_id_type=MESH)
     for b in range(4):
@@ -210,9 +236,9 @@
             start_own(b, j)
     exchange_in(cot, ct, 1)
 
-    for b in range(2):
-        for k in range(mp):
-            serve_item(b, 0, k)
+    ready = lag + 1
+    for t in range(mp + ready):
+        tick(t)
     own_hid.wait()
     exchange_wait(hid, xh, 0)
     length = lens[z]
@@ -255,9 +281,10 @@
 
     @pl.loop(0, pairs)
     def _(i):
-        for part in range(max(1, items // pairs)):
-            item = i * max(1, items // pairs) + part
-            serve_item(2, item // mp, item % mp)
+        @pl.when(i % (pairs // mp) == 0)
+        def _():
+            tick(mp + ready + i // (pairs // mp), mp + ready, 2 * mp + ready - 1)
+
         cols = pl.ds(pl.multiple_of(i * 128, 128), 128)
         q2 = qs[:, cols]
         k2 = ks[:, cols]
@@ -296,40 +323,33 @@
         acc[rows, :] = jnp.zeros((ROWS, width), F32)
 
     own_local(2).wait()
-    for j in range(2):
-        for k in range(mp):
-            sibling_done(2, j, k)
-
-    tiles = units // tile
-    early = mp
-
-    @pl.loop(0, tiles)
-    def _(i):
-        @pl.when(i % (tiles // early) == 0)
-        def _():
-            item = i // (tiles // early)
-            serve_item(3, item // mp, item % mp)
-
-        cols = pl.ds(pl.multiple_of(i * tile, tile), tile)
-        inner = dot(low[...], wu[:, cols]) + expand_bias[:, cols]
-        cdf = 0.5 * (1.0 + lax.erf(inner * math.sqrt(0.5)))
-        act[:, cols] = (inner * cdf).astype(BF16)
-        slope[:, cols] = (cdf + inner * (jnp.exp(-0.5 * inner * inner) * (1.0 / math.sqrt(2.0 * math.pi)))).astype(BF16)
+
+    def slab(i):
+        zz = (z + mp - i % mp) % mp
+        return pl.multiple_of(zz * cu + (i // mp) * hu, 128)
+
+    @pl.loop(0, items)
+    def _(i):
+        tick(2 * mp + ready + i, 2 * mp + ready, 4 * mp + ready - 1)
+        sibling_done(2, i // mp, i % mp)
+        base = slab(i)
+
+        @pl.loop(0, hu // tile)
+        def _(n):
+            cols = pl.ds(pl.multiple_of(base + n * tile, 128), tile)
+            inner = dot(low[...], wu[:, cols]) + expand_bias[:, cols]
+            cdf = 0.5 * (1.0 + lax.erf(inner * math.sqrt(0.5)))
+            act[:, cols] = (inner * cdf).astype(BF16)
+            bell = jnp.exp(-0.5 * inner * inner) * (1.0 / math.sqrt(2.0 * math.pi))
+            slope[:, cols] = (cdf + inner * bell).astype(BF16)
 
     own_local(3).wait()
 
     @pl.loop(0, items)
     def _(i):
-        @pl.when(i + early < items)
-        def _():
-            ahead = i + early
-            serve_item(3, ahead // mp, ahead % mp)
-
-        j = i // mp
-        k = i % mp
-        sibling_done(3, j, k)
-        zz = (z + mp - k) % mp
-        cols = pl.ds(pl.multiple_of(zz * cu + j * hu, 128), hu)
+        tick(4 * mp + ready + i, 4 * mp + ready, 6 * mp + ready - 1)
+        sibling_done(3, i // mp, i % mp)
+        cols = pl.ds(slab(i), hu)
 
         @pl.loop(0, width // 512)
         def _(n):
@@ -338,10 +358,8 @@
 
     own_cot.wait()
     exchange_wait(cot, ct, 1)
-    sum_ffn[...] = jnp.zeros_like(sum_ffn)
-    sum_down[...] = jnp.zeros_like(sum_down)
-    sum_attn[...] = jnp.zeros_like(sum_attn)
-    sum_out[...] = jnp.zeros_like(sum_out)
+    early[0] = jnp.zeros(early.shape[1:], F32)
+    late[0] = jnp.zeros(late.shape[1:], F32)
 
     @pl.loop(0, seq // ROWS)
     def _(i):
@@ -356,8 +374,8 @@
         g = inv * (e - row_mean(e) - norm * row_mean(e * norm))
         acc[rows, :] = g
         low[rows, :] = g.astype(BF16)
-        sum_ffn[...] += jnp.sum(dy, axis=0, keepdims=True)
-        sum_down[...] += jnp.sum(g, axis=0, keepdims=True)
+        early[0, 0:1, :] += jnp.sum(dy, axis=0, keepdims=True)
+        early[0, 1:2, :] += jnp.sum(g, axis=0, keepdims=True)
 
     def push_out(buf, dst, which, there):
         pltpu.make_async_remote_copy(
@@ -370,12 +388,15 @@
     keep_out = pltpu.make_async_copy(tokens(outb, z), out.at[z], local_sem.at[6])
     keep_out.start()
 
-    @pl.loop(0, tiles)
-    def _(i):
-        cols = pl.ds(pl.multiple_of(i * tile, tile), tile)
-        g = (dot(low[...], wd[:, cols]) * slope[:, cols].astype(F32)).astype(BF16)
-        act[:, cols] = g
-        sum_up[:, cols] = jnp.sum(g.astype(F32), axis=0, keepdims=True)
+    for part in range(units // width):
+
+        @pl.loop(0, width // tile)
+        def _(i):
+            here = pl.ds(pl.multiple_of(i * tile, tile), tile)
+            cols = pl.ds(pl.multiple_of(part * width + i * tile, tile), tile)
+            g = (dot(low[...], wd[:, cols]) * slope[:, cols].astype(F32)).astype(BF16)
+            act[:, cols] = g
+            early[0, 4 + part:5 + part, here] = jnp.sum(g.astype(F32), axis=0, keepdims=True)
 
     @pl.loop(0, width // tile)
     def _(i):
@@ -391,16 +412,37 @@
         first = inverse[rows, 0:1] * (e - row_mean(e) - norm * row_mean(e * norm))
         acc[rows, :] = first
         low[rows, :] = first.astype(BF16)
-        sum_attn[...] += jnp.sum(g, axis=0, keepdims=True)
-        sum_out[...] += jnp.sum(first, axis=0, keepdims=True)
+        early[0, 2:3, :] += jnp.sum(g, axis=0, keepdims=True)
+        early[0, 3:4, :] += jnp.sum(first, axis=0, keepdims=True)
 
     @pl.loop(0, width // tile)
     def _(i):
         cols = pl.ds(pl.multiple_of(i * tile, tile), tile)
         gctx[:, cols] = dot(low[...], wo[:, cols]).astype(BF16)
 
+    def sum_send_step(buf, which, s):
+        pltpu.make_async_remote_copy(
+            src_ref=buf.at[s], dst_ref=inbox.at[which, s], send_sem=sum_send.at[which, s],
+            recv_sem=sum_recv.at[which, s], device_id=peers[s], device_id_type=MESH,
+        ).start()
+
+    def sum_take_step(buf, which, s):
+        pltpu.make_async_copy(inbox.at[which, s], inbox.at[which, s], sum_recv.at[which, s]).wait()
+        buf[s + 1] = buf[s] + inbox[which, s]
+
+    steps = len(peers)
+    sum_send_step(early, 0, 0)
+
     @pl.loop(0, pairs)
     def _(i):
+        for s in range(steps):
+
+            @pl.when(i == min(s + 1, pairs - 1))
+            def _(s=s):
+                sum_take_step(early, 0, s)
+                if s + 1 < steps:
+                    sum_send_step(early, 0, s + 1)
+
         cols = pl.ds(pl.multiple_of(i * 128, 128), 128)
         q2 = qs[:, cols]
         k2t = ks[:, cols].T
@@ -420,9 +462,10 @@
         qs[:, cols] = dq2.astype(BF16)
         ks[:, cols] = jnp.where(lane < HEAD_DIM, dk[0], dk[1]).astype(BF16)
         vs[:, cols] = dv2
-        sum_q[:, cols] = jnp.sum(dq2, axis=0, keepdims=True)
-        sum_v[:, cols] = jnp.sum(dv2.astype(F32), axis=0, keepdims=True)
-
+        late[0, 0:1, cols] = jnp.sum(dq2, axis=0, keepdims=True)
+        late[0, 1:2, cols] = jnp.sum(dv2.astype(F32), axis=0, keepdims=True)
+
+    sum_send_step(late, 1, 0)
     side = seq // 2
     per = mp // 2
     mine = z // per
@@ -432,6 +475,14 @@
 
         @pl.loop(0, width // tile)
         def _(i):
+            for u in range(2):
+                s = 2 * turn + u
+
+                @pl.when(i == 2 * u + 1)
+                def _(s=s):
+                    sum_take_step(late, 1, s)
+                    sum_send_step(late, 1, s + 1)
+
             cols = pl.ds(pl.multiple_of(i * tile, tile), tile)
             x = acc[rows, cols]
             x += dot(qs[rows, :], wq[0, cols, :], NT)
@@ -445,6 +496,16 @@
                 push_out(xh, grad, 3, there)
     keep_grad = pltpu.make_async_copy(tokens(xh, z), grad.at[z], local_sem.at[7])
     keep_grad.start()
+
+    for s in range(4, steps):
+        sum_take_step(late, 1, s)
+        if s + 1 < steps:
+            sum_send_step(late, 1, s + 1)
+    sums[0] = early[steps]
+    sums[1] = late[steps]
+    for which, buf in ((0, early), (1, late)):
+        for s in range(steps):
+            pltpu.make_async_copy(buf.at[s], buf.at[s], sum_send.at[which, s]).wait()
 
     keep_out.wait()
     keep_grad.wait()
@@ -485,16 +546,17 @@
         v.reshape(1, -1)
         for v in (bias_q, bias_v, bias_out, expand_bias, bias_down, gain_attn, shift_attn, gain_ffn, shift_ffn)
     ]
-    vec = jax.ShapeDtypeStruct((1, width), F32)
+    steps = dp.bit_length() + mp.bit_length() - 2
+    summed = (4 + units // width, width)
     moved = jax.ShapeDtypeStruct(hidden_in.shape, BF16)
     ring = dp // 2
     sem = pltpu.SemaphoreType.DMA
     results = pl.pallas_call(
         functools.partial(step_kernel, (dp, mp, seq, width, units)),
         name="step",
-        out_shape=(moved, moved, vec, vec, vec, jax.ShapeDtypeStruct((1, units), F32), vec, vec, vec),
+        out_shape=(moved, moved, jax.ShapeDtypeStruct((2,) + summed, F32)),
         in_specs=[smem, smem] + [vmem] * 10 + [anys] * 6,
-        out_specs=(anys, anys) + (vmem,) * 7,
+        out_specs=(anys, anys, vmem),
         scratch_shapes=[
             pltpu.VMEM((3, width, width), BF16),
             pltpu.VMEM((width, width), BF16),
@@ -508,21 +570,26 @@
             pltpu.VMEM((seq, units), BF16),
             pltpu.VMEM((seq, units), BF16),
             pltpu.VMEM((seq, width), BF16),
+            pltpu.VMEM((steps + 1,) + summed, F32),
+            pltpu.VMEM((steps + 1,) + summed, F32),
+            pltpu.VMEM((2, steps) + summed, F32),
             sem((8,)),
             sem((6, mp, ring)),
             sem((6, mp)),
             sem((4, 4)),
             sem((4, mp)),
             sem((4, mp)),
+            sem((2, steps)),
+            sem((2, steps)),
         ],
         compiler_params=pltpu.CompilerParams(collective_id=0, has_side_effects=True, vmem_limit_bytes=67043328),
     )(
         lengths, separators, *rows, hidden_in, cotangent, jnp.swapaxes(query_key_value_weight, 0, 1),
         output_weight, up_weight, down_weight,
     )
-    factor = 1.0 / (here * seq * dp)
-    sums = lax.psum(tuple(s.reshape(-1) for s in results[2:]), ("dp", "mp"))
-    return results[:2] + tuple(s * factor for s in sums)
+    sums = results[2] * (1.0 / (here * seq * dp))
+    first, last = sums[0], sums[1]
+    return results[:2] + (last[0], last[1], first[3], first[4:].reshape(-1), first[1], first[2], first[0])
 
 
 def solution(mesh):

time: 349 us -> 232 us (0.66)
  Pallas kernels: 298 us -> 225 us
  blocking collectives: 43.9 us -> 0 us
    pallas_call x1, Pallas kernels: 298 us -> 225 us  [on_device(): pl.pallas_call(functools.partial(step_kernel, (dp, mp, seq, width, units)...]
    psum x1 -> x0, blocking collectives: 43.9 us -> none  [on_device(): sums = lax.psum(tuple((s.reshape(-1) for s in results[2:])), ('dp', 'mp'))]
where the time goes in v3:
time: 232 us; the launch traced here: 231 us
  Pallas kernels  225 us (97%)
  local copies, waits for them, and re-layouts  4.56 us (2%)
    pallas_call x1, Pallas kernels, on_device(): pl.pallas_call(functools.partial(step_kernel, (dp, mp, seq, width, units)...  225 us

profile of v3, /device:TPU:0, one launch (start us, length us, event | category | flops | bytes accessed | tf_op | source)
XLA Modules:
  0.0 231.0 jit_solution(5654928155354615167)
XLA Ops:
  0.6 224.9 %step.1 = (bf16[4,128,1024]{2,1,0:T(8,128)(2,1)}, bf16[4,128,1024]{2,1,0:T(8,128)(2,1)}, f32[2,8,1024]{2,1,0:T(8,128)}) custom-call(s32[4]{0:T(128)} %lens.1, s32[4]{0:T(128)} %seps.1, f32[2,1024]{1,0:T(2,128)} %seg.1, f32[1,1024]{1,0:T(1,128)} %bitcast.24, f32[1,1024]{1,0:T(1,128)} %bitcast.25, f32[1,1024]{1,0:T(1,128)} %bitcast.26, f32[1,4096]{1,0:T(1,128)} %bitcast.22, ...), custom_call_target="tpu_custom_call" | custom-call | tf_op jit(solution)/shard_map/step/pallas_call | solution.py:554
  225.6 0.8 broadcast_multiply_fusion
  226.4 0.6 fusion
  227.1 0.6 copy.29
  227.7 0.0 copy-start
  227.7 2.4 %copy.32 = bf16[4,128,1024]{2,1,0:T(8,128)(2,1)} copy(bf16[4,128,1024]{2,1,0:T(8,128)(2,1)} %get-tuple-element.30) | data formatting | bytes 2097152
  230.0 0.0 copy-done
  230.0 1.0 copy.33
  (1 shorter events, 0.0 us)
Async XLA Ops:
  227.7 2.4 %copy-start = (bf16[4,128,1024]{2,1,0:T(8,128)(2,1)S(1)}, bf16[4,128,1024]{2,1,0:T(8,128)(2,1)}, u32[]{:S(2)}) copy-start(bf16[4,128,1024]{2,1,0:T(8,128)(2,1)} %get-tuple-element.31) | copy-start | bytes 3145732

commit v4 on v3

--- a/solution.py
+++ b/solution.py
@@ -15,6 +15,12 @@
 MESH = pl.DeviceIdType.MESH
 ROWS = 64
 LAG = 0
+PLAN = {0: (1,), 3: (2,), 6: (3,), 9: (4,), 12: (5,)}
+HID_AT = {1: (1,2,3)}
+COT_AT = {16: (1,2,3)}
+QKV_TICKS = 2
+ATTN_TICKS = 4
+UP_TICKS = 6
 NN = ((1,), (0,))
 NT = ((1,), (1,))
 
@@ -75,9 +81,9 @@
     def piece(b, j):
         return (0, 1, 2, 4)[b] + j
 
-    def send(src, b, j, k, origin, way, target):
+    def send(src, b, j, k, origin, way, target, part=()):
         zz = (z + mp - k) % mp
-        dst = region(b, j, k, origin)
+        dst = region(b, j, k, origin).at[part] if part else region(b, j, k, origin)
         recv = sib_sem.at[piece(b, j), zz] if way == 2 else ici_sem.at[piece(b, j), zz, origin]
         pltpu.make_async_remote_copy(
             src_ref=src, dst_ref=dst, send_sem=send_sem.at[b, way], recv_sem=recv, device_id=target, device_id_type=MESH
@@ -95,9 +101,6 @@
         send(src, b, j, k, pos, 2, sibling)
 
     def start_own(b, j):
-        for hop in range(1, mp):
-            there = (z + hop) % mp
-            send_z(b, j, there)
         spread(own_shard(b, j), b, j, 0)
 
     def send_z(b, j, there):
@@ -116,58 +119,60 @@
         else:
             pl.when(cond)(fn)
 
+    def relay(ref, b, j, k, origin, way, target):
+        part = (slice(None),) * (b == 0) + (pl.ds(way * (rb // 2), rb // 2),)
+        send(ref.at[part], b, j, k, origin, way, target, part)
+
     def serve_ring(b, j, k, dist):
-        even, odd = k % 2 == 0, k % 2 == 1
-
-        def from_left():
-            origin = (pos + ring - dist) % ring
+        if dist == half:
+            origin = (pos + half) % ring
+            send(arrived(b, j, k, origin), b, j, k, origin, 2, sibling)
+            return
+        pass_on = relay if dist + 1 == half else send
+        for way, origin, target in ((0, (pos + ring - dist) % ring, right), (1, (pos + dist) % ring, left)):
             ref = arrived(b, j, k, origin)
-            if dist + 1 < half:
-                send(ref, b, j, k, origin, 0, right)
-            elif dist + 1 == half:
-                pick(even, lambda: send(ref, b, j, k, origin, 0, right))
+            pass_on(ref, b, j, k, origin, way, target)
             send(ref, b, j, k, origin, 2, sibling)
 
-        def from_right():
-            origin = (pos + dist) % ring
-            ref = arrived(b, j, k, origin)
-            if dist + 1 < half:
-                send(ref, b, j, k, origin, 1, left)
-            elif dist + 1 == half:
-                pick(odd, lambda: send(ref, b, j, k, origin, 1, left))
-            send(ref, b, j, k, origin, 2, sibling)
-
-        if dist < half:
-            from_left()
-            from_right()
-        else:
-            pick(even, from_left)
-            pick(odd, from_right)
-
-    total_items = 6 * mp
-    bounds = (0, mp, 2 * mp, 4 * mp, total_items)
+    pieces = ((0, 0), (1, 0), (2, 0), (2, 1), (3, 0), (3, 1))
+    order = [(b, j, 0) for b, j in pieces] + [(b, j, k) for b, j in pieces for k in range(1, mp)]
     lag = half + LAG
-
-    def with_item(u, low_u, high_u, fn):
-        if isinstance(u, int):
-            if 0 <= u < total_items:
-                b = sum(u >= x for x in bounds[1:4])
-                fn(b, (u - bounds[b]) // mp, (u - bounds[b]) % mp)
-            return
-        for b in range(4):
-            if low_u < bounds[b + 1] and high_u >= bounds[b]:
-                inside = True
-                if low_u < bounds[b]:
-                    inside = u >= bounds[b]
-                if high_u >= bounds[b + 1]:
-                    inside = (u < bounds[b + 1]) if inside is True else jnp.logical_and(inside, u < bounds[b + 1])
-                pick(inside, lambda b=b: fn(b, (u - bounds[b]) // mp, (u - bounds[b]) % mp))
-
-    def tick(t, low_t=0, high_t=0):
-        with_item(t, low_t, high_t, lambda b, j, k: pick(k > 0, lambda: serve_column(b, j, k)))
+    served = [0]
+
+    def with_item(t, fn):
+        if 0 <= t < len(order):
+            fn(*order[t])
+
+    def tick(t):
+        with_item(t, lambda b, j, k: k > 0 and serve_column(b, j, k))
         for dist in range(1, half + 1):
-            back = dist + LAG
-            with_item(t - back, low_t - back, high_t - back, lambda b, j, k: serve_ring(b, j, k, dist))
+            with_item(t - dist - LAG, lambda b, j, k: serve_ring(b, j, k, dist))
+
+    def column_out(p):
+        for hop in range(1, mp):
+            send_z(*pieces[p], (z + hop) % mp)
+
+    def serve_to(count):
+        for t in range(served[0], count):
+            for p in PLAN.get(t, ()):
+                column_out(p)
+            for hop in HID_AT.get(t, ()):
+                exchange_in(hid, xh, 0, hop)
+            for hop in COT_AT.get(t, ()):
+                exchange_in(cot, ct, 1, hop)
+            tick(t)
+        served[0] = max(served[0], count)
+
+    def whole_at(b, j, k):
+        return order.index((b, j, k)) + lag + 1
+
+    def serve_within(i, slots, until):
+        first = served[0]
+        for slot in range(slots):
+            upto = min(until(slot), len(order) + lag)
+            if upto > served[0]:
+                pl.when(i == slot)(functools.partial(serve_to, upto))
+                served[0] = max(served[0], upto)
 
     def sibling_done(b, j, k):
         zz = (z + mp - k) % mp
@@ -210,13 +215,12 @@
     own_cot.start()
     pl.semaphore_wait(barrier, len(partners))
 
-    def exchange_in(src, dst, which):
-        for hop in range(1, mp):
-            there = (z + hop) % mp
-            pltpu.make_async_remote_copy(
-                src_ref=src.at[there], dst_ref=tokens(dst, z), send_sem=row_send.at[which, there],
-                recv_sem=row_recv.at[which, z], device_id=(d, there), device_id_type=MESH,
-            ).start()
+    def exchange_in(src, dst, which, hop):
+        there = (z + hop) % mp
+        pltpu.make_async_remote_copy(
+            src_ref=src.at[there], dst_ref=tokens(dst, z), send_sem=row_send.at[which, there],
+            recv_sem=row_recv.at[which, z], device_id=(d, there), device_id_type=MESH,
+        ).start()
 
     def exchange_wait(src, dst, which):
         for hop in range(1, mp):
@@ -228,17 +232,11 @@
             there = (z + hop) % mp
             pltpu.make_async_copy(ref, ref, row_send.at[which, there]).wait()
 
-    start_own(0, 0)
-    exchange_in(hid, xh, 0)
-    start_own(1, 0)
-    for b in (2, 3):
-        for j in range(2):
-            start_own(b, j)
-    exchange_in(cot, ct, 1)
-
-    ready = lag + 1
-    for t in range(mp + ready):
-        tick(t)
+    column_out(0)
+    for p, (b, j) in enumerate(pieces):
+        start_own(b, j)
+
+    serve_to(whole_at(0, 0, mp - 1))
     own_hid.wait()
     exchange_wait(hid, xh, 0)
     length = lens[z]
@@ -265,6 +263,8 @@
 
     @pl.loop(0, width // tile)
     def _(i):
+        base_t = whole_at(0, 0, mp - 1)
+        serve_within(i, width // tile, lambda n: base_t + (n + 1) * QKV_TICKS // (width // tile))
         cols = pl.ds(pl.multiple_of(i * tile, tile), tile)
         qs[:, cols] = ((dot(low[...], wq[0, :, cols]) + bias_q[:, cols]) * scale).astype(BF16)
         ks[:, cols] = dot(low[...], wq[1, :, cols]).astype(BF16)
@@ -281,10 +281,8 @@
 
     @pl.loop(0, pairs)
     def _(i):
-        @pl.when(i % (pairs // mp) == 0)
-        def _():
-            tick(mp + ready + i // (pairs // mp), mp + ready, 2 * mp + ready - 1)
-
+        base_t = whole_at(0, 0, mp - 1) + QKV_TICKS
+        serve_within(i, pairs, lambda n: base_t + (n + 1) * ATTN_TICKS // pairs)
         cols = pl.ds(pl.multiple_of(i * 128, 128), 128)
         q2 = qs[:, cols]
         k2 = ks[:, cols]
@@ -301,6 +299,7 @@
         low[:, cols] = jnp.concatenate(ctxs, axis=0).T.astype(BF16)
 
     own_local(1).wait()
+    serve_to(whole_at(1, 0, mp - 1))
     for k in range(mp):
         sibling_done(1, 0, k)
 
@@ -323,6 +322,7 @@
         acc[rows, :] = jnp.zeros((ROWS, width), F32)
 
     own_local(2).wait()
+    AFTER_ATTN = served[0]
 
     def slab(i):
         zz = (z + mp - i % mp) % mp
@@ -330,7 +330,7 @@
 
     @pl.loop(0, items)
     def _(i):
-        tick(2 * mp + ready + i, 2 * mp + ready, 4 * mp + ready - 1)
+        serve_within(i, items, lambda n: max(whole_at(2, n // mp, n % mp), AFTER_ATTN + (n + 1) * UP_TICKS // items))
         sibling_done(2, i // mp, i % mp)
         base = slab(i)
 
@@ -347,7 +347,7 @@
 
     @pl.loop(0, items)
     def _(i):
-        tick(4 * mp + ready + i, 4 * mp + ready, 6 * mp + ready - 1)
+        serve_within(i, items, lambda n: max(whole_at(3, n // mp, n % mp), whole_at(3, 0, mp - 1) + n + 1))
         sibling_done(3, i // mp, i % mp)
         cols = pl.ds(slab(i), hu)
 

time: 232 us -> 218 us (0.940)
  Pallas kernels: 225 us -> 210 us
    pallas_call x1, Pallas kernels: 225 us -> 210 us  [on_device(): pl.pallas_call(functools.partial(step_kernel, (dp, mp, seq, width, units)...]
where the time goes in v4:
time: 218 us; the launch traced here: 216 us
  Pallas kernels  210 us (96%)
  local copies, waits for them, and re-layouts  4.56 us (2%)
    pallas_call x1, Pallas kernels, on_device(): pl.pallas_call(functools.partial(step_kernel, (dp, mp, seq, width, units)...  210 us

profile of v4, /device:TPU:0, one launch (start us, length us, event | category | flops | bytes accessed | tf_op | source)
XLA Modules:
  0.0 216.2 jit_solution(2496297948365408186)
XLA Ops:
  0.6 210.1 %step.1 = (bf16[4,128,1024]{2,1,0:T(8,128)(2,1)}, bf16[4,128,1024]{2,1,0:T(8,128)(2,1)}, f32[2,8,1024]{2,1,0:T(8,128)}) custom-call(s32[4]{0:T(128)} %lens.1, s32[4]{0:T(128)} %seps.1, f32[2,1024]{1,0:T(2,128)} %seg.1, f32[1,1024]{1,0:T(1,128)} %bitcast.24, f32[1,1024]{1,0:T(1,128)} %bitcast.25, f32[1,1024]{1,0:T(1,128)} %bitcast.26, f32[1,4096]{1,0:T(1,128)} %bitcast.22, ...), custom_call_target="tpu_custom_call" | custom-call | tf_op jit(solution)/shard_map/step/pallas_call | solution.py:554
  210.7 0.8 broadcast_multiply_fusion
  211.6 0.6 fusion
  212.2 0.6 copy.29
  212.8 0.0 copy-start
  212.8 2.4 %copy.32 = bf16[4,128,1024]{2,1,0:T(8,128)(2,1)} copy(bf16[4,128,1024]{2,1,0:T(8,128)(2,1)} %get-tuple-element.30) | data formatting | bytes 2097152
  215.2 0.0 copy-done
  215.2 1.0 copy.33
  (1 shorter events, 0.0 us)
Async XLA Ops:
  212.8 2.4 %copy-start = (bf16[4,128,1024]{2,1,0:T(8,128)(2,1)S(1)}, bf16[4,128,1024]{2,1,0:T(8,128)(2,1)}, u32[]{:S(2)}) copy-start(bf16[4,128,1024]{2,1,0:T(8,128)(2,1)} %get-tuple-element.31) | copy-start | bytes 3145732

commit v5 on v4

--- a/solution.py
+++ b/solution.py
@@ -430,18 +430,23 @@
         pltpu.make_async_copy(inbox.at[which, s], inbox.at[which, s], sum_recv.at[which, s]).wait()
         buf[s + 1] = buf[s] + inbox[which, s]
 
+    def sum_pass(buf, which, s):
+        if s < steps:
+            sum_take_step(buf, which, s)
+            if s + 1 < steps:
+                sum_send_step(buf, which, s + 1)
+
     steps = len(peers)
+    in_loop = min(steps, (pairs - 1) // 2)
     sum_send_step(early, 0, 0)
 
     @pl.loop(0, pairs)
     def _(i):
-        for s in range(steps):
-
-            @pl.when(i == min(s + 1, pairs - 1))
+        for s in range(in_loop):
+
+            @pl.when(i == 2 * s + 2)
             def _(s=s):
-                sum_take_step(early, 0, s)
-                if s + 1 < steps:
-                    sum_send_step(early, 0, s + 1)
+                sum_pass(early, 0, s)
 
         cols = pl.ds(pl.multiple_of(i * 128, 128), 128)
         q2 = qs[:, cols]
@@ -475,14 +480,6 @@
 
         @pl.loop(0, width // tile)
         def _(i):
-            for u in range(2):
-                s = 2 * turn + u
-
-                @pl.when(i == 2 * u + 1)
-                def _(s=s):
-                    sum_take_step(late, 1, s)
-                    sum_send_step(late, 1, s + 1)
-
             cols = pl.ds(pl.multiple_of(i * tile, tile), tile)
             x = acc[rows, cols]
             x += dot(qs[rows, :], wq[0, cols, :], NT)
@@ -490,6 +487,8 @@
             x += dot(vs[rows, :], wq[2, cols, :], NT)
             xh[rows, cols] = x.astype(BF16)
 
+        sum_pass(early, 0, in_loop + turn)
+        sum_pass(late, 1, turn)
         for q in range(per):
             there = block * per + (z + q + turn) % per
             if turn == 0 or q < per - 1:
@@ -497,10 +496,9 @@
     keep_grad = pltpu.make_async_copy(tokens(xh, z), grad.at[z], local_sem.at[7])
     keep_grad.start()
 
-    for s in range(4, steps):
-        sum_take_step(late, 1, s)
-        if s + 1 < steps:
-            sum_send_step(late, 1, s + 1)
+    for s in range(2, steps):
+        sum_pass(early, 0, in_loop + s)
+        sum_pass(late, 1, s)
     sums[0] = early[steps]
     sums[1] = late[steps]
     for which, buf in ((0, early), (1, late)):

time: 218 us -> 209 us (0.959)
  Pallas kernels: 210 us -> 201 us
    pallas_call x1, Pallas kernels: 210 us -> 201 us  [on_device(): pl.pallas_call(functools.partial(step_kernel, (dp, mp, seq, width, units)...]
where the time goes in v5:
time: 209 us; the launch traced here: 207 us
  Pallas kernels  201 us (96%)
  local copies, waits for them, and re-layouts  4.56 us (2%)
    pallas_call x1, Pallas kernels, on_device(): pl.pallas_call(functools.partial(step_kernel, (dp, mp, seq, width, units)...  201 us

profile of v5, /device:TPU:0, one launch (start us, length us, event | category | flops | bytes accessed | tf_op | source)
XLA Modules:
  0.0 207.1 jit_solution(2376750864646603436)
XLA Ops:
  0.6 201.0 %step.1 = (bf16[4,128,1024]{2,1,0:T(8,128)(2,1)}, bf16[4,128,1024]{2,1,0:T(8,128)(2,1)}, f32[2,8,1024]{2,1,0:T(8,128)}) custom-call(s32[4]{0:T(128)} %lens.1, s32[4]{0:T(128)} %seps.1, f32[2,1024]{1,0:T(2,128)} %seg.1, f32[1,1024]{1,0:T(1,128)} %bitcast.24, f32[1,1024]{1,0:T(1,128)} %bitcast.25, f32[1,1024]{1,0:T(1,128)} %bitcast.26, f32[1,4096]{1,0:T(1,128)} %bitcast.22, ...), custom_call_target="tpu_custom_call" | custom-call | tf_op jit(solution)/shard_map/step/pallas_call | solution.py:552
  201.7 0.8 broadcast_multiply_fusion
  202.5 0.6 fusion
  203.2 0.6 copy.29
  203.8 0.0 copy-start
  203.8 2.4 %copy.32 = bf16[4,128,1024]{2,1,0:T(8,128)(2,1)} copy(bf16[4,128,1024]{2,1,0:T(8,128)(2,1)} %get-tuple-element.30) | data formatting | bytes 2097152
  206.1 0.0 copy-done
  206.1 1.0 copy.33
  (1 shorter events, 0.0 us)
Async XLA Ops:
  203.8 2.4 %copy-start = (bf16[4,128,1024]{2,1,0:T(8,128)(2,1)S(1)}, bf16[4,128,1024]{2,1,0:T(8,128)(2,1)}, u32[]{:S(2)}) copy-start(bf16[4,128,1024]{2,1,0:T(8,128)(2,1)} %get-tuple-element.31) | copy-start | bytes 3145732

commit v6 on v5

--- a/solution.py
+++ b/solution.py
@@ -15,11 +15,11 @@
 MESH = pl.DeviceIdType.MESH
 ROWS = 64
 LAG = 0
+PRE_TICKS = 13
 PLAN = {0: (1,), 3: (2,), 6: (3,), 9: (4,), 12: (5,)}
 HID_AT = {1: (1,2,3)}
-COT_AT = {16: (1,2,3)}
-QKV_TICKS = 2
-ATTN_TICKS = 4
+COT_AT = {19: (1,2,3)}
+ATTN_TICKS = 6
 UP_TICKS = 6
 NN = ((1,), (0,))
 NT = ((1,), (1,))
@@ -236,7 +236,7 @@
     for p, (b, j) in enumerate(pieces):
         start_own(b, j)
 
-    serve_to(whole_at(0, 0, mp - 1))
+    serve_to(PRE_TICKS)
     own_hid.wait()
     exchange_wait(hid, xh, 0)
     length = lens[z]
@@ -256,20 +256,7 @@
         low[rows, :] = embed(rows, first).astype(BF16)
 
     own_local(0).wait()
-    for k in range(mp):
-        sibling_done(0, 0, k)
-
     tile = 256
-
-    @pl.loop(0, width // tile)
-    def _(i):
-        base_t = whole_at(0, 0, mp - 1)
-        serve_within(i, width // tile, lambda n: base_t + (n + 1) * QKV_TICKS // (width // tile))
-        cols = pl.ds(pl.multiple_of(i * tile, tile), tile)
-        qs[:, cols] = ((dot(low[...], wq[0, :, cols]) + bias_q[:, cols]) * scale).astype(BF16)
-        ks[:, cols] = dot(low[...], wq[1, :, cols]).astype(BF16)
-        vs[:, cols] = (dot(low[...], wq[2, :, cols]) + bias_v[:, cols]).astype(BF16)
-
     pairs = heads // 2
     lane = lax.broadcasted_iota(jnp.int32, (seq, 2 * HEAD_DIM), 1)
 
@@ -279,10 +266,14 @@
 
     items = 2 * mp
 
-    @pl.loop(0, pairs)
-    def _(i):
-        base_t = whole_at(0, 0, mp - 1) + QKV_TICKS
-        serve_within(i, pairs, lambda n: base_t + (n + 1) * ATTN_TICKS // pairs)
+    share = pairs // mp
+    spots = mp * (share + 1)
+
+    def attn_until(n):
+        paced = PRE_TICKS + (n + 1) * ATTN_TICKS // spots
+        return max(paced, whole_at(0, 0, n // (share + 1)))
+
+    def attend(i):
         cols = pl.ds(pl.multiple_of(i * 128, 128), 128)
         q2 = qs[:, cols]
         k2 = ks[:, cols]
@@ -296,7 +287,25 @@
             p = (e * (1.0 / jnp.sum(e, axis=0, keepdims=True))).astype(BF16)
             probs[2 * i + hh] = p
             ctxs.append(dot(v2t[hh * HEAD_DIM:(hh + 1) * HEAD_DIM], p))
-        low[:, cols] = jnp.concatenate(ctxs, axis=0).T.astype(BF16)
+        gctx[:, cols] = jnp.concatenate(ctxs, axis=0).T.astype(BF16)
+
+    @pl.loop(0, spots)
+    def _(spot):
+        serve_within(spot, spots, attn_until)
+        k = spot // (share + 1)
+        own = (z + mp - k) % mp
+
+        @pl.when(spot % (share + 1) == 0)
+        def _():
+            sibling_done(0, 0, k)
+            cols = pl.ds(pl.multiple_of(own * cq, 128), cq)
+            qs[:, cols] = ((dot(low[...], wq[0, :, cols]) + bias_q[:, cols]) * scale).astype(BF16)
+            ks[:, cols] = dot(low[...], wq[1, :, cols]).astype(BF16)
+            vs[:, cols] = (dot(low[...], wq[2, :, cols]) + bias_v[:, cols]).astype(BF16)
+
+        @pl.when(spot % (share + 1) > 0)
+        def _():
+            attend(own * share + spot % (share + 1) - 1)
 
     own_local(1).wait()
     serve_to(whole_at(1, 0, mp - 1))
@@ -306,7 +315,7 @@
     @pl.loop(0, width // tile)
     def _(i):
         cols = pl.ds(pl.multiple_of(i * tile, tile), tile)
-        acc[:, cols] = dot(low[...], wo[cols, :], NT)
+        acc[:, cols] = dot(gctx[...], wo[cols, :], NT)
 
     @pl.loop(0, seq // ROWS)
     def _(i):
@@ -388,19 +397,20 @@
     keep_out = pltpu.make_async_copy(tokens(outb, z), out.at[z], local_sem.at[6])
     keep_out.start()
 
+    wide = 512
     for part in range(units // width):
 
-        @pl.loop(0, width // tile)
+        @pl.loop(0, width // wide)
         def _(i):
-            here = pl.ds(pl.multiple_of(i * tile, tile), tile)
-            cols = pl.ds(pl.multiple_of(part * width + i * tile, tile), tile)
+            here = pl.ds(pl.multiple_of(i * wide, wide), wide)
+            cols = pl.ds(pl.multiple_of(part * width + i * wide, wide), wide)
             g = (dot(low[...], wd[:, cols]) * slope[:, cols].astype(F32)).astype(BF16)
             act[:, cols] = g
             early[0, 4 + part:5 + part, here] = jnp.sum(g.astype(F32), axis=0, keepdims=True)
 
-    @pl.loop(0, width // tile)
-    def _(i):
-        cols = pl.ds(pl.multiple_of(i * tile, tile), tile)
+    @pl.loop(0, width // wide)
+    def _(i):
+        cols = pl.ds(pl.multiple_of(i * wide, wide), wide)
         acc[:, cols] += dot(act[...], wu[cols, :], NT)
 
     @pl.loop(0, seq // ROWS)
@@ -415,9 +425,9 @@
         early[0, 2:3, :] += jnp.sum(g, axis=0, keepdims=True)
         early[0, 3:4, :] += jnp.sum(first, axis=0, keepdims=True)
 
-    @pl.loop(0, width // tile)
-    def _(i):
-        cols = pl.ds(pl.multiple_of(i * tile, tile), tile)
+    @pl.loop(0, width // wide)
+    def _(i):
+        cols = pl.ds(pl.multiple_of(i * wide, wide), wide)
         gctx[:, cols] = dot(low[...], wo[:, cols]).astype(BF16)
 
     def sum_send_step(buf, which, s):
@@ -478,9 +488,9 @@
         block = 1 - mine if turn == 0 else mine
         rows = pl.ds(pl.multiple_of(block * side, side), side)
 
-        @pl.loop(0, width // tile)
+        @pl.loop(0, width // wide)
         def _(i):
-            cols = pl.ds(pl.multiple_of(i * tile, tile), tile)
+            cols = pl.ds(pl.multiple_of(i * wide, wide), wide)
             x = acc[rows, cols]
             x += dot(qs[rows, :], wq[0, cols, :], NT)
             x += dot(ks[rows, :], wq[1, cols, :], NT)

time: 209 us -> 208 us (level)
  no operation moved by 1% of the time
where the time goes in v6:
time: 208 us; the launch traced here: 205 us
  Pallas kernels  199 us (96%)
  local copies, waits for them, and re-layouts  4.56 us (2%)
    pallas_call x1, Pallas kernels, on_device(): pl.pallas_call(functools.partial(step_kernel, (dp, mp, seq, width, units)...  199 us

profile of v6, /device:TPU:0, one launch (start us, length us, event | category | flops | bytes accessed | tf_op | source)
XLA Modules:
  0.0 205.0 jit_solution(5798602162684370969)
XLA Ops:
  0.6 198.9 %step.1 = (bf16[4,128,1024]{2,1,0:T(8,128)(2,1)}, bf16[4,128,1024]{2,1,0:T(8,128)(2,1)}, f32[2,8,1024]{2,1,0:T(8,128)}) custom-call(s32[4]{0:T(128)} %lens.1, s32[4]{0:T(128)} %seps.1, f32[2,1024]{1,0:T(2,128)} %seg.1, f32[1,1024]{1,0:T(1,128)} %bitcast.24, f32[1,1024]{1,0:T(1,128)} %bitcast.25, f32[1,1024]{1,0:T(1,128)} %bitcast.26, f32[1,4096]{1,0:T(1,128)} %bitcast.22, ...), custom_call_target="tpu_custom_call" | custom-call | tf_op jit(solution)/shard_map/step/pallas_call | solution.py:562
  199.6 0.8 broadcast_multiply_fusion
  200.5 0.6 fusion
  201.1 0.6 copy.29
  201.7 0.0 copy-start
  201.7 2.4 %copy.32 = bf16[4,128,1024]{2,1,0:T(8,128)(2,1)} copy(bf16[4,128,1024]{2,1,0:T(8,128)(2,1)} %get-tuple-element.30) | data formatting | bytes 2097152
  204.0 0.0 copy-done
  204.0 1.0 copy.33
  (1 shorter events, 0.0 us)
Async XLA Ops:
  201.7 2.4 %copy-start = (bf16[4,128,1024]{2,1,0:T(8,128)(2,1)S(1)}, bf16[4,128,1024]{2,1,0:T(8,128)(2,1)}, u32[]{:S(2)}) copy-start(bf16[4,128,1024]{2,1,0:T(8,128)(2,1)} %get-tuple-element.31) | copy-start | bytes 3145732
